TPU v7x, 32 devices: a whole 2x2x4 slice. The times are simulated.
32 devices in a mesh: freq: 2 (over x), row: 16 (over z, y, core).
Axes of the slice: x: 2, y: 2, z: 4, core: 2. Of those that a mesh axis runs over, the one named last changes fastest.
Arguments:
- data_real: bfloat16 [16384, 8192], P(('freq', 'row')), parts along dimension 0, may hold values from -6 to 6
- data_imag: bfloat16 [16384, 8192], P(('freq', 'row')), parts along dimension 0, may hold values from -6 to 6
- counts: int32 [8, 8], replicated, may hold values from 0 to 4
- source_cols: int32 [128], replicated, may hold values from 0 to 8191, as said below
Outputs:
- pred_real: float32 [16384, 128], P(('freq', 'row')), parts along dimension 0
- pred_imag: float32 [16384, 128], P(('freq', 'row')), parts along dimension 0
There are 2 independent parts, one for each index of `freq`. A program takes and returns all parts, laid end to end along the dimension named above; an argument that names none is the same for every part. Nothing has to cross between parts.
Inputs may be any that keep to these rules, and one draw needn't show every extreme that they name: `source_cols`: 128 distinct grid points; 0 and 8191 are always among them.
All inputs are finite; a program needn't handle non-finite values.
Results may differ from a plain program's by a relative error of at most 0.0029.
Values may be sent and summed in bfloat16 or wider, within the bound.
A program may use at most 128 MiB of HBM per device.

v0:
```python
import math

import jax
import jax.numpy as jnp
from jax import lax
from jax.sharding import PartitionSpec as P

TILES = 8


def tile_weights(counts, row_ids, width):
    tile = width // TILES
    onehot = (row_ids[:, None] // tile == jnp.arange(TILES, dtype=jnp.int32)[None, :]).astype(
        jnp.float32
    )
    table = counts.astype(jnp.float32)
    forward = jnp.dot(onehot, table, precision=lax.Precision.HIGHEST)
    backward = jnp.dot(onehot, table.T, precision=lax.Precision.HIGHEST)
    height = row_ids.shape[0]
    forward = jnp.broadcast_to(forward[:, :, None], (height, TILES, tile)).reshape(height, width)
    backward = jnp.broadcast_to(backward[:, :, None], (height, TILES, tile)).reshape(height, width)
    return (forward, backward)


def complex_pair(left_real, left_imag, right_real, right_imag, dims):
    dot_rr = lax.dot_general(left_real, right_real, dims, preferred_element_type=jnp.float32)
    dot_ii = lax.dot_general(left_imag, right_imag, dims, preferred_element_type=jnp.float32)
    dot_ri = lax.dot_general(left_real, right_imag, dims, preferred_element_type=jnp.float32)
    dot_ir = lax.dot_general(left_imag, right_real, dims, preferred_element_type=jnp.float32)
    return jnp.concatenate([dot_rr - dot_ii, dot_ri + dot_ir], axis=1)


def shards(data_real, data_imag, counts, source_cols):
    rows, width = data_real.shape
    mirror_real, mirror_imag = (
        lax.all_to_all(data_real, "row", split_axis=1, concat_axis=0, tiled=True),
        lax.all_to_all(data_imag, "row", split_axis=1, concat_axis=0, tiled=True),
    )
    row_ids = lax.axis_index("row") * rows + jnp.arange(rows, dtype=jnp.int32)
    forward, backward = tile_weights(counts, row_ids, width)
    denom = jnp.maximum(forward + backward, 1.0)
    sym_real = (
        (forward * data_real.astype(jnp.float32) + backward * mirror_real.T.astype(jnp.float32))
        / denom
    ).astype(jnp.bfloat16)
    sym_imag = (
        (forward * data_imag.astype(jnp.float32) + backward * mirror_imag.T.astype(jnp.float32))
        / denom
    ).astype(jnp.bfloat16)
    panel_real = jnp.take(sym_real, source_cols, axis=1)
    panel_imag = jnp.take(sym_imag, source_cols, axis=1)
    sources = source_cols.shape[0]
    factor = -1.0 / math.sqrt(width)
    piece_real = lax.all_gather(panel_real, "row", axis=0, tiled=True)
    piece_imag = lax.all_gather(panel_imag, "row", axis=0, tiled=True)
    summed = complex_pair(sym_real, sym_imag, piece_real, piece_imag, (((1,), (0,)), ((), ())))
    predicted = factor * summed
    return (predicted[:, :sources], predicted[:, sources:])


def solution(mesh):
    placed = (P(("freq", "row"), None), P(("freq", "row"), None), P(), P())
    return jax.shard_map(
        shards,
        mesh=mesh,
        in_specs=placed,
        out_specs=(P(("freq", "row"), None), P(("freq", "row"), None)),
        check_vma=False,
    )
```

profile of v0, /device:TPU:0, one launch (start us, length us, event | category | flops | bytes accessed | tf_op | source)
XLA Modules:
  0.0 530.0 jit_solution(13418963480100498488)
XLA Ops:
  7.2 7.5 %copy.17 = bf16[64,16,8,512]{3,2,0,1:T(8,128)(2,1)} copy(bf16[64,16,8,512]{3,2,1,0:T(8,128)(2,1)} %bitcast.68) | data formatting | bytes 16777216 | tf_op jit(solution)/shard_map/all_to_all | solution.py:36
  14.7 7.4 %all-to-all-start = ((bf16[512,16,512]{2,0,1:T(8,128)(2,1)}), bf16[512,16,512]{2,0,1:T(8,128)(2,1)}, u32[]{:S(2)}, u32[]{:S(2)}) async-start(bf16[512,16,512]{2,0,1:T(8,128)(2,1)} %bitcast.71), calls=%async_computation | async-start | bytes 16777216 | tf_op jit(solution)/shard_map/all_to_all | solution.py:36
  22.1 7.5 %copy.16 = bf16[64,16,8,512]{3,2,0,1:T(8,128)(2,1)} copy(bf16[64,16,8,512]{3,2,1,0:T(8,128)(2,1)} %bitcast.69) | data formatting | bytes 16777216 | tf_op jit(solution)/shard_map/all_to_all | solution.py:37
  29.7 143.2 %all-to-all-done = bf16[512,16,512]{2,0,1:T(8,128)(2,1)} async-done(((bf16[512,16,512]{2,0,1:T(8,128)(2,1)}), bf16[512,16,512]{2,0,1:T(8,128)(2,1)}, u32[]{:S(2)}, u32[]{:S(2)}) %all-to-all-start) | async-done | bytes 8388640 | tf_op jit(solution)/shard_map/all_to_all | solution.py:36
  172.8 36.5 %all-to-all-start.1 = ((bf16[512,16,512]{2,0,1:T(8,128)(2,1)}), bf16[512,16,512]{2,0,1:T(8,128)(2,1)}, u32[]{:S(2)}, u32[]{:S(2)}) async-start(bf16[512,16,512]{2,0,1:T(8,128)(2,1)} %bitcast.70), calls=%async_computation.1 | async-start | bytes 16777216 | tf_op jit(solution)/shard_map/all_to_all | solution.py:37
  209.4 0.0 all-gather.3.cloned.1.call-start
  209.5 12.0 %copy.6 = bf16[512,8192]{0,1:T(8,128)(2,1)} copy(bf16[512,8192]{1,0:T(8,128)(2,1)} %param.6) | data formatting | bytes 16777216 | tf_op args[0]
  221.4 0.0 copy-start.3
  221.5 0.0 copy-start.2
  221.5 11.5 %copy.8 = bf16[512,8192]{0,1:T(8,128)(2,1)} copy(bf16[512,8192]{1,0:T(8,128)(2,1)} %param.7) | data formatting | bytes 16777216 | tf_op args[1]
  233.0 0.0 copy-done.3
  233.0 0.0 copy-done.2
  233.0 0.3 fusion.7
  233.3 0.3 fusion.8
  233.7 126.5 %all-to-all-done.1 = bf16[512,16,512]{2,0,1:T(8,128)(2,1)} async-done(((bf16[512,16,512]{2,0,1:T(8,128)(2,1)}), bf16[512,16,512]{2,0,1:T(8,128)(2,1)}, u32[]{:S(2)}, u32[]{:S(2)}) %all-to-all-start.1) | async-done | bytes 8388640 | tf_op jit(solution)/shard_map/all_to_all | solution.py:37
  360.1 18.6 %fusion.2 = (bf16[512,8192]{0,1:T(8,128)(2,1)}, bf16[512,8192]{0,1:T(8,128)(2,1)}) fusion(bf16[512,8192]{0,1:T(8,128)(2,1)} %copy.6, f32[512,8]{0,1:T(8,128)S(1)} %fusion.7, f32[512,8]{0,1:T(8,128)S(1)} %fusion.8, bf16[512,16,512]{2,0,1:T(8,128)(2,1)} %all-to-all-done, bf16[512,16,512]{2,0,1:T(8,128)(2,1)} %all-to-all-done.1, bf16[512,8192]{0,1:T(8,128)(2,1)} %copy.8), kind=kLoop, calls=%fused_computation.9 | loop fusion | flops 67108864 | bytes 50364416 | tf_op jit(solution)/shard_map/convert_element_type | solution.py:45
  378.7 5.3 %gather_fusion = bf16[128,512]{1,0:T(8,128)(2,1)S(1)} fusion(bf16[512,8192]{0,1:T(8,128)(2,1)} %get-tuple-element.7, s32[1024]{0:T(1024)S(1)} %pad_clamp_fusion), kind=kCustom, calls=%fused_computation.clone | custom fusion | bytes 262656 | tf_op jit(solution)/shard_map/jit(_take)/gather | solution.py:50
  384.0 5.3 %gather_fusion.1 = bf16[128,512]{1,0:T(8,128)(2,1)S(1)} fusion(bf16[512,8192]{0,1:T(8,128)(2,1)} %get-tuple-element.8, s32[1024]{0:T(1024)S(1)} %pad_clamp_fusion), kind=kCustom, calls=%fused_computation.1.clone | custom fusion | bytes 262656 | tf_op jit(solution)/shard_map/jit(_take)/gather | solution.py:51
  389.3 0.8 select_bitcast_fusion.1
  390.1 0.0 all-gather.3.cloned.1.call-update
  390.2 0.2 all-gather.5.cloned.1.call-start
  390.4 0.5 all-gather.5.cloned.1.call-update
  390.9 72.4 %all-gather.3.cloned.1.call-done = bf16[8192,128]{0,1:T(8,128)(2,1)} async-done(((bf16[512,128]{0,1:T(8,128)(2,1)}), bf16[8192,128]{0,1:T(8,128)(2,1)}) %all-gather.3.cloned.1.call-update) | async-done | bytes 2097168 | tf_op jit(solution)/shard_map/all_gather | solution.py:54
  463.3 5.3 fusion.17
  468.6 37.6 %all-gather.5.cloned.1.call-done = bf16[8192,128]{0,1:T(8,128)(2,1)} async-done(((bf16[512,128]{0,1:T(8,128)(2,1)}), bf16[8192,128]{0,1:T(8,128)(2,1)}) %all-gather.5.cloned.1.call-update) | async-done | bytes 2097168 | tf_op jit(solution)/shard_map/all_gather | solution.py:55
  506.2 0.0 copy-start.1
  506.2 5.4 %fusion.18 = f32[512,128]{0,1:T(8,128)S(1)} fusion(bf16[8192,128]{0,1:T(8,128)(2,1)} %all-gather.5.cloned.1.call-done, bf16[512,8192]{0,1:T(8,128)(2,1)} %get-tuple-element.7), kind=kOutput, calls=%fused_computation.42 | convolution fusion | flops 1073741824 | bytes 10747904 | tf_op jit(solution)/shard_map/dot_general | solution.py:28
  511.6 0.0 copy-done.1
  511.6 0.0 copy-start
  511.6 4.9 convolution_subtract_fusion
  516.6 0.0 copy-done
  516.6 4.8 convolution_add_fusion
  521.3 0.1 maximum_multiply_fusion
  521.5 0.8 copy.10
  522.3 0.8 copy.11
  (5 shorter events, 0.1 us)
Async XLA Ops:
  14.7 158.2 %all-to-all-start = ((bf16[512,16,512]{2,0,1:T(8,128)(2,1)}), bf16[512,16,512]{2,0,1:T(8,128)(2,1)}, u32[]{:S(2)}, u32[]{:S(2)}) async-start(bf16[512,16,512]{2,0,1:T(8,128)(2,1)} %bitcast.71), calls=%async_computation | async-start | bytes 16777216 | tf_op jit(solution)/shard_map/all_to_all | solution.py:36
  172.8 187.3 %all-to-all-start.1 = ((bf16[512,16,512]{2,0,1:T(8,128)(2,1)}), bf16[512,16,512]{2,0,1:T(8,128)(2,1)}, u32[]{:S(2)}, u32[]{:S(2)}) async-start(bf16[512,16,512]{2,0,1:T(8,128)(2,1)} %bitcast.70), calls=%async_computation.1 | async-start | bytes 16777216 | tf_op jit(solution)/shard_map/all_to_all | solution.py:37
  209.4 253.9 %all-gather.3.cloned.1.call-start = ((), (), s32[]{:S(2)}) async-start(), calls=%async_computation.2 | async-start | bytes 2228224 | tf_op jit(solution)/shard_map/all_gather | solution.py:54
  221.4 11.5 %copy-start.3 = (s32[128]{0:T(128)S(1)}, s32[128]{0:T(128)}, u32[]{:S(2)}) copy-start(s32[128]{0:T(128)} %param.9) | copy-start | bytes 1540
  221.5 11.6 %copy-start.2 = (s32[8,8]{1,0:T(8,128)S(1)}, s32[8,8]{1,0:T(8,128)}, u32[]{:S(2)}) copy-start(s32[8,8]{1,0:T(8,128)} %param.8) | copy-start | bytes 772
  390.2 116.0 %all-gather.5.cloned.1.call-start = ((), (), s32[]{:S(2)}) async-start(), calls=%async_computation.3 | async-start | bytes 2228224 | tf_op jit(solution)/shard_map/all_gather | solution.py:55
  506.2 5.4 %copy-start.1 = (bf16[8192,128]{0,1:T(8,128)(2,1)S(1)}, bf16[8192,128]{0,1:T(8,128)(2,1)}, u32[]{:S(2)}) copy-start(bf16[8192,128]{0,1:T(8,128)(2,1)} %all-gather.5.cloned.1.call-done) | copy-start | bytes 6291460
  511.6 4.9 copy-start
Sparse Core Ops, SparseCore 0:
  390.3 72.9 all-gather.2
  466.0 40.1 all-gather.4
where the time goes:
time: 531 us; the launch traced here: 530 us
  waiting for transfers between devices  380 us (72%)
  local copies, waits for them, and re-layouts  50.9 us (10%)
  starting transfers between devices  44.2 us (8%)
  matrix products  21 us (4%)
  other arithmetic  19.4 us (4%)
  between operations  14.2 us (3%)
    all_to_all x1, waiting for transfers between devices, shards(): lax.all_to_all(data_real, 'row', split_axis=1, concat_axis=0, tiled=True)  143 us
    all_to_all x1, waiting for transfers between devices, shards(): lax.all_to_all(data_imag, 'row', split_axis=1, concat_axis=0, tiled=True)  126 us
    all_gather x1, waiting for transfers between devices, shards(): piece_real = lax.all_gather(panel_real, 'row', axis=0, tiled=True)  72.4 us
    all_gather x1, waiting for transfers between devices, shards(): piece_imag = lax.all_gather(panel_imag, 'row', axis=0, tiled=True)  37.6 us
    all_to_all x1, starting transfers between devices, shards(): lax.all_to_all(data_imag, 'row', split_axis=1, concat_axis=0, tiled=True)  36.5 us
    unnamed x12, local copies, waits for them, and re-layouts  25.2 us
    convert_element_type x1, other arithmetic, shards(): sym_real = ((forward * data_real.astype(jnp.float32) + backward * mirror_...  18.6 us
  transfers between devices with their start and end apart: 4, of which 4 were waited for; matrix products, arithmetic and copies ran while one was open for 7% of the time, Pallas kernels for 0%

commit v1 on v0

v1 whole, which is shorter than its diff:
```python
import functools
import math

import jax
import jax.numpy as jnp
from jax import lax
from jax.experimental import pallas as pl
from jax.experimental.pallas import tpu as pltpu
from jax.sharding import PartitionSpec as P

TILES = 8
SEND = jnp.float32
NT = (((1,), (1,)), ((), ()))
NN = (((1,), (0,)), ((), ()))


def dot(a, b, dims=NN):
    return lax.dot_general(a, b, dims, preferred_element_type=jnp.float32)


def pick_kernel(row0_ref, cols_ref, dr_ref, di_ref, rows_ref, own_ref):
    j = pl.program_id(0)
    height, width = dr_ref.shape
    cols = cols_ref[...]
    sources = cols.shape[0]
    at_row = row0_ref[0] + lax.broadcasted_iota(jnp.int32, (sources, height), 1)
    pick_rows = (cols == at_row).astype(jnp.float32).astype(jnp.bfloat16)
    at_col = j * width + lax.broadcasted_iota(jnp.int32, (sources, width), 1)
    pick_cols = (cols == at_col).astype(jnp.float32).astype(jnp.bfloat16)
    dr = dr_ref[...]
    di = di_ref[...]
    rows_ref[0, :sources, :] = dot(pick_rows, dr).astype(jnp.bfloat16)
    rows_ref[0, sources:, :] = dot(pick_rows, di).astype(jnp.bfloat16)

    @pl.when(j == 0)
    def _():
        own_ref[...] = jnp.zeros_like(own_ref)

    own_ref[:sources, :] += dot(pick_cols, dr, NT)
    own_ref[sources:, :] += dot(pick_cols, di, NT)


def turned(panel):
    half = panel.shape[0] // 2
    return jnp.concatenate([-panel[half:], panel[:half]], axis=0)


def back_kernel(scale_ref, panel_ref, dr_ref, di_ref, out_ref):
    j = pl.program_id(0)
    panel = panel_ref[...]
    total = dot(panel, dr_ref[...]) + dot(turned(panel), di_ref[...])
    out_ref[0] = (scale_ref[j] * total).astype(out_ref.dtype)


def front_kernel(scale_ref, panels_ref, back_ref, dr_ref, di_ref, real_ref, imag_ref, acc, *, factor):
    j = pl.program_id(0)

    @pl.when(j == 0)
    def _():
        acc[...] = jnp.zeros_like(acc)

    panel = panels_ref[0]
    acc[...] += scale_ref[j] * (dot(dr_ref[...], panel, NT) + dot(di_ref[...], turned(panel), NT))

    @pl.when(j == pl.num_programs(0) - 1)
    def _():
        total = factor * (acc[...] + back_ref[0].astype(jnp.float32).T)
        half = total.shape[1] // 2
        real_ref[...] = total[:, :half]
        imag_ref[...] = total[:, half:]


def shards(n, data_real, data_imag, counts, source_cols):
    rows, width = data_real.shape
    sources = source_cols.shape[0]
    tile = width // TILES
    factor = -1.0 / math.sqrt(width)
    me = lax.axis_index("row")
    row0 = me * rows
    table = counts.astype(jnp.float32)
    forward = lax.dynamic_index_in_dim(table, row0 // tile, 0, keepdims=False)
    backward = lax.dynamic_index_in_dim(table, row0 // tile, 1, keepdims=False)
    denom = jnp.maximum(forward + backward, 1.0)
    scale = jnp.repeat(forward / denom, n // TILES)
    smem = pl.BlockSpec(memory_space=pltpu.SMEM)
    whole = lambda shape: pl.BlockSpec(shape, lambda j: (0,) * len(shape))
    block = pl.BlockSpec((rows, rows), lambda j: (0, j))
    params = pltpu.CompilerParams(vmem_limit_bytes=48 << 20)
    picked, own = pl.pallas_call(
        pick_kernel,
        grid=(n,),
        out_shape=(
            jax.ShapeDtypeStruct((n, 2 * sources, rows), jnp.bfloat16),
            jax.ShapeDtypeStruct((2 * sources, rows), jnp.float32),
        ),
        in_specs=[smem, whole((sources, 1)), block, block],
        out_specs=(
            pl.BlockSpec((1, 2 * sources, rows), lambda j: (j, 0, 0)),
            whole((2 * sources, rows)),
        ),
        compiler_params=params,
    )(row0.reshape(1), source_cols.reshape(sources, 1), data_real, data_imag)
    mirror = lax.psum_scatter(picked, "row", scatter_dimension=0, tiled=True)[0]
    tiles = source_cols // tile
    w = jnp.tile(forward[tiles], 2)[:, None]
    v = jnp.tile(backward[tiles], 2)[:, None]
    panel = ((w * own + v * mirror.astype(jnp.float32)) / jnp.maximum(w + v, 1.0)).astype(jnp.bfloat16)
    panels = lax.all_gather(panel, "row", axis=0, tiled=False)
    back = pl.pallas_call(
        back_kernel,
        grid=(n,),
        out_shape=jax.ShapeDtypeStruct((n, 2 * sources, rows), SEND),
        in_specs=[smem, whole((2 * sources, rows)), block, block],
        out_specs=pl.BlockSpec((1, 2 * sources, rows), lambda j: (j, 0, 0)),
        compiler_params=params,
    )(scale, panel, data_real, data_imag)
    back = lax.psum_scatter(back, "row", scatter_dimension=0, tiled=True)
    return pl.pallas_call(
        functools.partial(front_kernel, factor=factor),
        grid=(n,),
        out_shape=(jax.ShapeDtypeStruct((rows, sources), jnp.float32),) * 2,
        in_specs=[
            smem,
            pl.BlockSpec((1, 2 * sources, rows), lambda j: (j, 0, 0)),
            whole((1, 2 * sources, rows)),
            block,
            block,
        ],
        out_specs=(whole((rows, sources)),) * 2,
        scratch_shapes=[pltpu.VMEM((rows, 2 * sources), jnp.float32)],
        compiler_params=params,
    )(scale, panels, back, data_real, data_imag)


def generic(data_real, data_imag, counts, source_cols):
    rows, width = data_real.shape
    sources = source_cols.shape[0]
    tile = width // TILES
    factor = -1.0 / math.sqrt(width)
    row0 = lax.axis_index("row") * rows
    table = counts.astype(jnp.float32)
    forward = lax.dynamic_index_in_dim(table, row0 // tile, 0, keepdims=False)
    backward = lax.dynamic_index_in_dim(table, row0 // tile, 1, keepdims=False)
    scale = jnp.repeat(forward / jnp.maximum(forward + backward, 1.0), tile)
    at_row = row0 + jnp.arange(rows, dtype=jnp.int32)
    pick_rows = (source_cols[:, None] == at_row[None, :]).astype(jnp.bfloat16)
    tn = (((0,), (1,)), ((), ()))
    picked = jnp.concatenate([dot(data_real, pick_rows, tn), dot(data_imag, pick_rows, tn)], axis=1)
    mirror = lax.psum_scatter(picked.astype(jnp.bfloat16), "row", scatter_dimension=0, tiled=True)
    own = jnp.concatenate([jnp.take(data_real, source_cols, axis=1), jnp.take(data_imag, source_cols, axis=1)], axis=1)
    tiles = source_cols // tile
    w = jnp.tile(forward[tiles], 2)[None, :]
    v = jnp.tile(backward[tiles], 2)[None, :]
    panel = (w * own.astype(jnp.float32) + v * mirror.astype(jnp.float32)) / jnp.maximum(w + v, 1.0)
    panel = panel.astype(jnp.bfloat16)
    swap = lambda p: jnp.concatenate([-p[:, sources:], p[:, :sources]], axis=1)
    panels = lax.all_gather(panel, "row", axis=0, tiled=True)
    tt = (((0,), (0,)), ((), ()))
    back = scale[:, None] * (dot(data_real, panel, tt) + dot(data_imag, swap(panel), tt))
    back = lax.psum_scatter(back, "row", scatter_dimension=0, tiled=True)
    steps = jnp.stack([
        s * (
            dot(data_real[:, t * tile : (t + 1) * tile], panels[t * tile : (t + 1) * tile])
            + dot(data_imag[:, t * tile : (t + 1) * tile], swap(panels[t * tile : (t + 1) * tile]))
        )
        for t, s in enumerate(scale[::tile])
    ])
    total = factor * (steps.sum(0) + back)
    return total[:, :sources], total[:, sources:]


def solution(mesh):
    n = mesh.shape["row"]

    def body(data_real, data_imag, counts, source_cols):
        rows = data_real.shape[0]
        if rows % 128 == 0 and n % TILES == 0:
            return shards(n, data_real, data_imag, counts, source_cols)
        return generic(data_real, data_imag, counts, source_cols)

    placed = (P(("freq", "row"), None), P(("freq", "row"), None), P(), P())
    return jax.shard_map(
        body,
        mesh=mesh,
        in_specs=placed,
        out_specs=(P(("freq", "row"), None), P(("freq", "row"), None)),
        check_vma=False,
    )
```

time: 531 us -> 290 us (0.55)
  waiting for transfers between devices: 380 us -> 204 us
  Pallas kernels: 0 us -> 50 us
  starting transfers between devices: 44.2 us -> 0.12 us
  local copies, waits for them, and re-layouts: 50.9 us -> 8.52 us
  matrix products: 21 us -> 0 us
  other arithmetic: 19.4 us -> 11.9 us
    all_to_all x2 -> x0, waiting for transfers between devices: 270 us -> none  [the longest x1 143 us: shards(): lax.all_to_all(data_real, 'row', split_axis=1, concat_axis=0, tiled=True)]
    reduce_scatter x0 -> x2, waiting for transfers between devices: none -> 171 us  [the longest x1 108 us: shards(): back = lax.psum_scatter(back, 'row', scatter_dimension=0, tiled=True)]
    all_gather x2 -> x1, waiting for transfers between devices: 110 us -> 32.8 us  [shards(): panels = lax.all_gather(panel, 'row', axis=0, tiled=False)]
    pallas_call x0 -> x3, Pallas kernels: none -> 50 us  [the longest x1 17.6 us: shards(): pl.pallas_call(pick_kernel, grid=(n,), out_shape=(jax.ShapeDtypeStruct((n...]
    all_to_all x2 -> x0, starting transfers between devices: 44 us -> none  [the longest x1 36.5 us: shards(): lax.all_to_all(data_imag, 'row', split_axis=1, concat_axis=0, tiled=True)]
    dot_general x6 -> x0, matrix products: 21 us -> none  [the longest x1 5.42 us: complex_pair(): lax.dot_general(left_real, right_imag, dims, preferred_element_type=jnp.f...]
    unnamed x12, local copies, waits for them, and re-layouts: 25.2 us -> 6.13 us
    convert_element_type x1 -> x2, other arithmetic: 18.6 us -> 1.84 us  [the longest x1 1.83 us: shards(): ((w * own + v * mirror.astype(jnp.float32)) / jnp.maximum(w + v, 1.0)).as...]
  transfers between devices with their start and end apart: 4 -> 3, of which waited for: 4 -> 3; matrix products, arithmetic and copies ran while one was open for 7% -> 4% of each run, Pallas kernels for 0% -> 6%
where the time goes in v1:
time: 290 us; the launch traced here: 289 us
  waiting for transfers between devices  204 us (70%)
  Pallas kernels  50 us (17%)
  between operations  13.8 us (5%)
  other arithmetic  11.9 us (4%)
  local copies, waits for them, and re-layouts  8.52 us (3%)
    reduce_scatter x1, waiting for transfers between devices, shards(): back = lax.psum_scatter(back, 'row', scatter_dimension=0, tiled=True)  108 us
    reduce_scatter x1, waiting for transfers between devices, shards(): mirror = lax.psum_scatter(picked, 'row', scatter_dimension=0, tiled=True)[0]  63.7 us
    all_gather x1, waiting for transfers between devices, shards(): panels = lax.all_gather(panel, 'row', axis=0, tiled=False)  32.8 us
    pallas_call x1, Pallas kernels, shards(): pl.pallas_call(pick_kernel, grid=(n,), out_shape=(jax.ShapeDtypeStruct((n...  17.6 us
    pallas_call x1, Pallas kernels, shards(): pl.pallas_call(back_kernel, grid=(n,), out_shape=jax.ShapeDtypeStruct((n,...  16.7 us
    pallas_call x1, Pallas kernels, shards(): pl.pallas_call(functools.partial(front_kernel, factor=factor), grid=(n,),...  15.7 us
    gather x1, other arithmetic, shards(): w = jnp.tile(forward[tiles], 2)[:, None]  10.1 us
    unnamed x12, local copies, waits for them, and re-layouts  6.13 us
  transfers between devices with their start and end apart: 3, of which 3 were waited for; matrix products, arithmetic and copies ran while one was open for 4% of the time, Pallas kernels for 6%

profile of v1, /device:TPU:0, one launch (start us, length us, event | category | flops | bytes accessed | tf_op | source)
XLA Modules:
  0.0 288.6 jit_solution(16944891740431215087)
XLA Ops:
  7.2 0.0 reduce-scatter.3.cloned.1.call-start
  7.2 0.8 copy.7.cols_ref
  8.0 0.0 copy-start.4
  8.0 0.0 copy-start.5
  8.0 17.6 %shard_map.59 = (bf16[16,256,512]{2,1,0:T(8,128)(2,1)S(1)}, f32[256,512]{1,0:T(8,128)S(1)}) custom-call(s32[1]{0:T(128)} %bitcast.10.row0_ref, s32[128,1]{1,0:T(8,128)S(1)} %copy.7.cols_ref, bf16[512,8192]{1,0:T(8,128)(2,1)} %dr_ref.5, bf16[512,8192]{1,0:T(8,128)(2,1)} %di_ref.5), custom_call_target="tpu_custom_call" | custom-call | tf_op jit(solution)/shard_map/pallas_call | solution.py:89
  25.6 0.0 copy-start
  25.6 1.9 copy-done
  27.5 0.0 reduce-scatter.3.cloned.1.call-update
  27.5 0.0 all-gather.3.cloned.1.call-start
  27.6 0.0 copy-done.4
  27.6 0.2 fusion.4
  27.8 0.7 fusion.6
  28.5 0.6 fusion.5
  29.1 0.0 copy-done.5
  29.1 10.1 %compare_select_fusion.5 = (f32[128]{0:T(128)S(1)}, f32[128]{0:T(128)S(1)}) fusion(f32[]{:T(128)} %bitcast.1, f32[]{:T(128)} %bitcast.2, f32[]{:T(128)} %bitcast.3, f32[]{:T(128)} %bitcast.4, f32[]{:T(128)} %bitcast.5, f32[]{:T(128)} %bitcast.6, f32[]{:T(128)} %bitcast.7, f32[]{:T(128)} %bitcast.8, s32[128]{0:T(128)S(1)} %copy-done.5, f32[]{:T(128)} %bitcast.19, ...), kind=kLoop, calls=%fused_computation.10 | loop fusion | flops 4992 | bytes 1600 | tf_op jit(solution)/shard_map/gather | solution.py:105
  39.2 63.7 %reduce-scatter.3.cloned.1.call-done = bf16[1,256,512]{2,1,0:T(8,128)(2,1)} async-done(((bf16[16,256,512]{2,1,0:T(8,128)(2,1)}), bf16[1,256,512]{2,1,0:T(8,128)(2,1)}) %reduce-scatter.3.cloned.1.call-update) | async-done | bytes 262160 | tf_op jit(solution)/shard_map/reduce_scatter | solution.py:103
  102.9 1.8 fusion.2.panel_ref
  104.7 0.0 all-gather.3.cloned.1.call-update
  104.8 0.0 reduce-scatter.5.cloned.1.call-start
  104.8 0.1 broadcast_in_dim.7
  104.9 0.1 reshape.33.scale_ref
  105.0 0.0 copy-start.2
  105.0 1.0 copy-done.2
  105.9 16.7 %shard_map.60 = f32[16,256,512]{2,1,0:T(8,128)} custom-call(f32[16]{0:T(128)S(1)} %reshape.33.scale_ref, bf16[256,512]{1,0:T(8,128)(2,1)S(1)} %copy-done.2, bf16[512,8192]{1,0:T(8,128)(2,1)} %dr_ref.5, bf16[512,8192]{1,0:T(8,128)(2,1)} %di_ref.5), custom_call_target="tpu_custom_call" | custom-call | tf_op jit(solution)/shard_map/pallas_call | solution.py:109
  122.6 0.0 reduce-scatter.5.cloned.1.call-update
  122.6 32.8 %all-gather.3.cloned.1.call-done = bf16[4096,512]{1,0:T(8,128)(2,1)} async-done(((bf16[256,512]{1,0:T(8,128)(2,1)}), bf16[4096,512]{1,0:T(8,128)(2,1)}) %all-gather.3.cloned.1.call-update) | async-done | bytes 4194320 | tf_op jit(solution)/shard_map/all_gather | solution.py:108
  155.4 107.8 %reduce-scatter.5.cloned.1.call-done.back_ref = f32[1,256,512]{2,1,0:T(8,128)} async-done(((f32[16,256,512]{2,1,0:T(8,128)}), f32[1,256,512]{2,1,0:T(8,128)}) %reduce-scatter.5.cloned.1.call-update) | async-done | bytes 524304 | tf_op jit(solution)/shard_map/reduce_scatter | solution.py:117
  263.1 0.0 copy-start.1
  263.1 2.2 copy-done.1
  265.3 0.0 copy-start.3
  265.3 1.0 copy-done.3
  266.4 15.7 %shard_map.61 = (f32[512,128]{1,0:T(8,128)}, f32[512,128]{1,0:T(8,128)}) custom-call(f32[16]{0:T(128)S(1)} %reshape.33.scale_ref, bf16[16,256,512]{2,1,0:T(8,128)(2,1)S(1)} %bitcast.35, f32[1,256,512]{2,1,0:T(8,128)S(1)} %copy-done.3, bf16[512,8192]{1,0:T(8,128)(2,1)} %dr_ref.5, bf16[512,8192]{1,0:T(8,128)(2,1)} %di_ref.5), custom_call_target="tpu_custom_call" | custom-call | tf_op jit(solution)/shard_map/pallas_call | solution.py:118
  (4 shorter events, 0.0 us)
Async XLA Ops:
  7.2 95.7 %reduce-scatter.3.cloned.1.call-start = ((), (), s32[]{:S(2)}) async-start(), calls=%async_computation.2 | async-start | bytes 4456448 | tf_op jit(solution)/shard_map/reduce_scatter | solution.py:103
  8.0 19.6 %copy-start.4 = (s32[8,8]{1,0:T(8,128)S(1)}, s32[8,8]{1,0:T(8,128)}, u32[]{:S(2)}) copy-start(s32[8,8]{1,0:T(8,128)} %param.6) | copy-start | bytes 772
  8.0 21.1 %copy-start.5 = (s32[128]{0:T(128)S(1)}, s32[128]{0:T(128)}, u32[]{:S(2)}) copy-start(s32[128]{0:T(128)} %param.7) | copy-start | bytes 1540
  25.6 1.9 copy-start
  27.5 127.8 %all-gather.3.cloned.1.call-start = ((), (), s32[]{:S(2)}) async-start(), calls=%async_computation.4 | async-start | bytes 4456448 | tf_op jit(solution)/shard_map/all_gather | solution.py:108
  104.8 158.4 %reduce-scatter.5.cloned.1.call-start = ((), (), s32[]{:S(2)}) async-start(), calls=%async_computation.3 | async-start | bytes 8912896 | tf_op jit(solution)/shard_map/reduce_scatter | solution.py:117
  105.0 1.0 copy-start.2
  263.1 2.2 copy-start.1
  265.3 1.0 copy-start.3
Sparse Core Ops, SparseCore 0:
  27.7 75.1 reduce-scatter.2
  105.9 49.4 all-gather.2
  160.0 103.0 reduce-scatter.4

commit v2 on v1

v2 whole, which is shorter than its diff:
```python
import functools
import math

import jax
import jax.numpy as jnp
from jax import lax
from jax.experimental import pallas as pl
from jax.experimental.pallas import tpu as pltpu
from jax.sharding import PartitionSpec as P

TILES = 8
NT = (((1,), (1,)), ((), ()))
NN = (((1,), (0,)), ((), ()))


def dot(a, b, dims=NN):
    return lax.dot_general(a, b, dims, preferred_element_type=jnp.float32)


def pick_kernel(info_ref, cols_ref, dr_ref, di_ref, rows_ref, own_ref):
    k = pl.program_id(0)
    height, width = dr_ref.shape
    cols = cols_ref[...]
    sources = cols.shape[0]
    at_row = info_ref[1] + lax.broadcasted_iota(jnp.int32, (sources, height), 1)
    pick_rows = (cols == at_row).astype(jnp.float32).astype(jnp.bfloat16)
    at_col = (2 * k + info_ref[0]) * width + lax.broadcasted_iota(jnp.int32, (sources, width), 1)
    pick_cols = (cols == at_col).astype(jnp.float32).astype(jnp.bfloat16)
    dr = dr_ref[...]
    di = di_ref[...]
    rows_ref[0, :sources, :] = dot(pick_rows, dr).astype(jnp.bfloat16)
    rows_ref[0, sources:, :] = dot(pick_rows, di).astype(jnp.bfloat16)

    @pl.when(k == 0)
    def _():
        own_ref[...] = jnp.zeros_like(own_ref)

    own_ref[:sources, :] += dot(pick_cols, dr, NT)
    own_ref[sources:, :] += dot(pick_cols, di, NT)


def turned(panel):
    half = panel.shape[0] // 2
    return jnp.concatenate([-panel[half:], panel[:half]], axis=0)


def back_kernel(info_ref, scale_ref, panel_ref, dr_ref, di_ref, out_ref):
    j = 2 * pl.program_id(0) + info_ref[0]
    panel = panel_ref[...]
    total = dot(panel, dr_ref[...]) + dot(turned(panel), di_ref[...])
    out_ref[0] = (scale_ref[j] * total).astype(out_ref.dtype)


def front_kernel(scale_ref, panels_ref, dr_ref, di_ref, out_ref):
    j = pl.program_id(0)

    @pl.when(j == 0)
    def _():
        out_ref[...] = jnp.zeros_like(out_ref)

    panel = panels_ref[0]
    out_ref[...] += scale_ref[j] * (dot(dr_ref[...], panel, NT) + dot(di_ref[...], turned(panel), NT))


def final_kernel(front_ref, first_ref, second_ref, real_ref, imag_ref, *, factor):
    sources = first_ref.shape[0]
    real_ref[...] = factor * (front_ref[:, :sources] + first_ref[...].T)
    imag_ref[...] = factor * (front_ref[:, sources:] + second_ref[...].T)


def swap(x, bit):
    n = lax.axis_size("row")
    return lax.ppermute(x, "row", [(i, i ^ (1 << bit)) for i in range(n)])


def halved(x, me, bit, axis):
    mine = (me >> bit) & 1
    got = swap(lax.dynamic_index_in_dim(x, 1 - mine, axis, False).astype(jnp.bfloat16), bit)
    return lax.dynamic_index_in_dim(x, mine, axis, False) + got.astype(x.dtype)


def scattered(kept, got, me):
    half = kept.shape[1] // 2
    total = kept + got.astype(kept.dtype)
    first = total[:, :half].reshape((2, 2, 2) + (half, kept.shape[2]))
    second = total[:, half:].reshape((2, 2, 2) + (half, kept.shape[2]))
    first = halved(first, me, 1, 2)
    second = halved(second, me, 2, 1)
    first = halved(first, me, 2, 1)
    second = halved(second, me, 3, 0)
    first = halved(first, me, 3, 0)
    second = halved(second, me, 1, 0)
    return first, second


def shards(n, data_real, data_imag, counts, source_cols):
    rows, width = data_real.shape
    sources = source_cols.shape[0]
    pair = 2 * sources
    tile = width // TILES
    factor = -1.0 / math.sqrt(width)
    me = lax.axis_index("row")
    core = me & 1
    row0 = me * rows
    table = counts.astype(jnp.float32)
    forward = lax.dynamic_index_in_dim(table, row0 // tile, 0, keepdims=False)
    backward = lax.dynamic_index_in_dim(table, row0 // tile, 1, keepdims=False)
    denom = jnp.maximum(forward + backward, 1.0)
    scale = jnp.repeat(forward / denom, n // TILES)
    smem = pl.BlockSpec(memory_space=pltpu.SMEM)
    params = pltpu.CompilerParams(vmem_limit_bytes=32 << 20)
    cost = pl.CostEstimate(flops=2 * rows * width * pair, bytes_accessed=4 * rows * width, transcendentals=0)
    half_cost = pl.CostEstimate(flops=rows * width * pair, bytes_accessed=2 * rows * width, transcendentals=0)
    whole = lambda shape: pl.BlockSpec(shape, lambda j, *refs: (0,) * len(shape))
    strided = pl.BlockSpec((rows, rows), lambda k, info: (0, 2 * k + info[0]))
    stacked = pl.BlockSpec((1, pair, rows), lambda k, *refs: (k, 0, 0))
    cols = source_cols.reshape(sources, 1)

    def pick(target):
        return pl.pallas_call(
            pick_kernel,
            grid_spec=pltpu.PrefetchScalarGridSpec(
                num_scalar_prefetch=1,
                grid=(n // 2,),
                in_specs=[whole((sources, 1)), strided, strided],
                out_specs=(stacked, whole((pair, rows))),
            ),
            out_shape=(
                jax.ShapeDtypeStruct((n // 2, pair, rows), jnp.bfloat16),
                jax.ShapeDtypeStruct((pair, rows), jnp.float32),
            ),
            compiler_params=params,
            cost_estimate=half_cost,
        )(jnp.stack([target, row0]), cols, data_real, data_imag)

    def back(target, kind, panel):
        return pl.pallas_call(
            back_kernel,
            grid_spec=pltpu.PrefetchScalarGridSpec(
                num_scalar_prefetch=1,
                grid=(n // 2,),
                in_specs=[smem, whole((pair, rows)), strided, strided],
                out_specs=stacked,
            ),
            out_shape=jax.ShapeDtypeStruct((n // 2, pair, rows), kind),
            compiler_params=params,
            cost_estimate=half_cost,
        )(target.reshape(1), scale, panel, data_real, data_imag)

    sent, own_a = pick(1 - core)
    got = swap(sent, 0)
    kept, own_b = pick(core)
    own = own_a + own_b
    tiles = (source_cols // tile)[:, None] == jnp.arange(TILES, dtype=jnp.int32)[None, :]
    w = jnp.tile(jnp.sum(jnp.where(tiles, forward, 0.0), axis=1), 2)[:, None]
    v = jnp.tile(jnp.sum(jnp.where(tiles, backward, 0.0), axis=1), 2)[:, None]
    mirror = jnp.concatenate(scattered(kept, got, me), axis=0).astype(jnp.float32)
    panel = ((w * own + v * mirror) / jnp.maximum(w + v, 1.0)).astype(jnp.bfloat16)
    panels = lax.all_gather(panel, "row", axis=0, tiled=False)
    sent = back(1 - core, jnp.bfloat16, panel)
    got = swap(sent, 0)
    kept = back(core, jnp.float32, panel)
    first, second = scattered(kept, got, me)
    front = pl.pallas_call(
        front_kernel,
        grid=(n,),
        out_shape=jax.ShapeDtypeStruct((rows, pair), jnp.float32),
        in_specs=[
            smem,
            stacked,
            pl.BlockSpec((rows, rows), lambda j: (0, j)),
            pl.BlockSpec((rows, rows), lambda j: (0, j)),
        ],
        out_specs=whole((rows, pair)),
        compiler_params=params,
        cost_estimate=cost,
    )(scale, panels, data_real, data_imag)
    return pl.pallas_call(
        functools.partial(final_kernel, factor=factor),
        out_shape=(jax.ShapeDtypeStruct((rows, sources), jnp.float32),) * 2,
        compiler_params=params,
    )(front, first, second)


def generic(data_real, data_imag, counts, source_cols):
    rows, width = data_real.shape
    sources = source_cols.shape[0]
    tile = width // TILES
    factor = -1.0 / math.sqrt(width)
    row0 = lax.axis_index("row") * rows
    table = counts.astype(jnp.float32)
    forward = lax.dynamic_index_in_dim(table, row0 // tile, 0, keepdims=False)
    backward = lax.dynamic_index_in_dim(table, row0 // tile, 1, keepdims=False)
    scale = jnp.repeat(forward / jnp.maximum(forward + backward, 1.0), tile)
    at_row = row0 + jnp.arange(rows, dtype=jnp.int32)
    pick_rows = (source_cols[:, None] == at_row[None, :]).astype(jnp.bfloat16)
    tn = (((0,), (1,)), ((), ()))
    picked = jnp.concatenate([dot(data_real, pick_rows, tn), dot(data_imag, pick_rows, tn)], axis=1)
    mirror = lax.psum_scatter(picked.astype(jnp.bfloat16), "row", scatter_dimension=0, tiled=True)
    own = jnp.concatenate([jnp.take(data_real, source_cols, axis=1), jnp.take(data_imag, source_cols, axis=1)], axis=1)
    tiles = source_cols // tile
    w = jnp.tile(forward[tiles], 2)[None, :]
    v = jnp.tile(backward[tiles], 2)[None, :]
    panel = (w * own.astype(jnp.float32) + v * mirror.astype(jnp.float32)) / jnp.maximum(w + v, 1.0)
    panel = panel.astype(jnp.bfloat16)
    swap = lambda p: jnp.concatenate([-p[:, sources:], p[:, :sources]], axis=1)
    panels = lax.all_gather(panel, "row", axis=0, tiled=True)
    tt = (((0,), (0,)), ((), ()))
    back = scale[:, None] * (dot(data_real, panel, tt) + dot(data_imag, swap(panel), tt))
    back = lax.psum_scatter(back, "row", scatter_dimension=0, tiled=True)
    steps = jnp.stack([
        s * (
            dot(data_real[:, t * tile : (t + 1) * tile], panels[t * tile : (t + 1) * tile])
            + dot(data_imag[:, t * tile : (t + 1) * tile], swap(panels[t * tile : (t + 1) * tile]))
        )
        for t, s in enumerate(scale[::tile])
    ])
    total = factor * (steps.sum(0) + back)
    return total[:, :sources], total[:, sources:]


def solution(mesh):
    n = mesh.shape["row"]

    def body(data_real, data_imag, counts, source_cols):
        rows = data_real.shape[0]
        if rows % 128 == 0 and n == 16:
            return shards(n, data_real, data_imag, counts, source_cols)
        return generic(data_real, data_imag, counts, source_cols)

    placed = (P(("freq", "row"), None), P(("freq", "row"), None), P(), P())
    return jax.shard_map(
        body,
        mesh=mesh,
        in_specs=placed,
        out_specs=(P(("freq", "row"), None), P(("freq", "row"), None)),
        check_vma=False,
    )
```

time: 290 us -> 182 us (0.63)
  waiting for transfers between devices: 204 us -> 71.2 us
  local copies, waits for them, and re-layouts: 8.52 us -> 32.5 us
  starting transfers between devices: 0.12 us -> 22.2 us
  Pallas kernels: 50 us -> 36.1 us
  other arithmetic: 11.9 us -> 4.9 us
    reduce_scatter x2 -> x0, waiting for transfers between devices: 171 us -> none  [the longest x1 108 us: shards(): back = lax.psum_scatter(back, 'row', scatter_dimension=0, tiled=True)]
    ppermute x0 -> x14, waiting for transfers between devices: none -> 71.2 us  [swap(): return lax.ppermute(x, 'row', [(i, i ^ 1 << bit) for i in range(n)])]
    all_gather x1, waiting for transfers between devices: 32.8 us -> 0.02 us  [shards(): panels = lax.all_gather(panel, 'row', axis=0, tiled=False)]
    unnamed x12 -> x26, local copies, waits for them, and re-layouts: 6.13 us -> 30.2 us
    ppermute x0 -> x14, starting transfers between devices: none -> 22.2 us  [swap(): return lax.ppermute(x, 'row', [(i, i ^ 1 << bit) for i in range(n)])]
    pallas_call x3 -> x6, Pallas kernels: 50 us -> 36.1 us  [the longest x2 15.8 us: pick(): pl.pallas_call(pick_kernel, grid_spec=pltpu.PrefetchScalarGridSpec(num_sc...]
    gather x1 -> x0, other arithmetic: 10.1 us -> none  [shards(): w = jnp.tile(forward[tiles], 2)[:, None]]
    add x0 -> x14, other arithmetic: none -> 3.79 us  [the longest x2 3.05 us: scattered(): total = kept + got.astype(kept.dtype)]
  transfers between devices with their start and end apart: 3 -> 15, of which waited for: 3 -> 9; matrix products, arithmetic and copies ran while one was open for 4% -> 2% of each run, Pallas kernels for 6% -> 10%
where the time goes in v2:
time: 182 us; the launch traced here: 181 us
  waiting for transfers between devices  71.2 us (39%)
  Pallas kernels  36.1 us (20%)
  local copies, waits for them, and re-layouts  32.5 us (18%)
  starting transfers between devices  22.2 us (12%)
  between operations  14.4 us (8%)
  other arithmetic  4.9 us (3%)
    ppermute x14, waiting for transfers between devices, swap(): return lax.ppermute(x, 'row', [(i, i ^ 1 << bit) for i in range(n)])  71.2 us
    unnamed x26, local copies, waits for them, and re-layouts  30.2 us
    ppermute x14, starting transfers between devices, swap(): return lax.ppermute(x, 'row', [(i, i ^ 1 << bit) for i in range(n)])  22.2 us
    pallas_call x2, Pallas kernels, pick(): pl.pallas_call(pick_kernel, grid_spec=pltpu.PrefetchScalarGridSpec(num_sc...  15.8 us
    pallas_call x1, Pallas kernels, shards(): pl.pallas_call(front_kernel, grid=(n,), out_shape=jax.ShapeDtypeStruct((r...  9.8 us
    pallas_call x2, Pallas kernels, back(): pl.pallas_call(back_kernel, grid_spec=pltpu.PrefetchScalarGridSpec(num_sc...  9.59 us
  transfers between devices with their start and end apart: 15, of which 9 were waited for; matrix products, arithmetic and copies ran while one was open for 2% of the time, Pallas kernels for 10%

profile of v2, /device:TPU:0, one launch (start us, length us, event | category | flops | bytes accessed | tf_op | source)
XLA Modules:
  0.0 181.3 jit_solution(7960591923216425351)
XLA Ops:
  7.2 0.0 all-gather.3.cloned.1.call-start
  7.2 0.8 copy.15.cols_ref
  8.0 0.1 pad_add_fusion
  8.1 3.4 %copy-done = bf16[512,8192]{1,0:T(8,128)(2,1)S(1)} copy-done((bf16[512,8192]{1,0:T(8,128)(2,1)S(1)}, bf16[512,8192]{1,0:T(8,128)(2,1)}, u32[]{:S(2)}) %copy-start) | copy-done | bytes 8388632
  11.4 3.4 %copy-done.4 = bf16[512,8192]{1,0:T(8,128)(2,1)S(1)} copy-done((bf16[512,8192]{1,0:T(8,128)(2,1)S(1)}, bf16[512,8192]{1,0:T(8,128)(2,1)}, u32[]{:S(2)}) %copy-start.4) | copy-done | bytes 8388632
  14.8 7.9 %shard_map.59 = (bf16[8,256,512]{2,1,0:T(8,128)(2,1)S(1)}, f32[256,512]{1,0:T(8,128)S(1)}) custom-call(s32[2]{0:T(128)S(1)} %get-tuple-element.18.info_ref, s32[128,1]{1,0:T(8,128)S(1)} %copy.15.cols_ref, bf16[512,8192]{1,0:T(8,128)(2,1)S(1)} %copy-done, bf16[512,8192]{1,0:T(8,128)(2,1)S(1)} %copy-done.4), custom_call_target="tpu_custom_call" | custom-call | flops 1073741824 | bytes 8388608 | tf_op jit(solution)/shard_map/pallas_call | solution.py:120
  22.7 0.5 collective-permute-start
  23.2 0.2 fusion.6
  23.4 3.4 %copy-done.1 = bf16[512,8192]{1,0:T(8,128)(2,1)S(1)} copy-done((bf16[512,8192]{1,0:T(8,128)(2,1)S(1)}, bf16[512,8192]{1,0:T(8,128)(2,1)}, u32[]{:S(2)}) %copy-start.1) | copy-done | bytes 8388632
  26.8 3.4 %copy-done.5 = bf16[512,8192]{1,0:T(8,128)(2,1)S(1)} copy-done((bf16[512,8192]{1,0:T(8,128)(2,1)S(1)}, bf16[512,8192]{1,0:T(8,128)(2,1)}, u32[]{:S(2)}) %copy-start.5) | copy-done | bytes 8388632
  30.2 7.9 %shard_map.60 = (bf16[8,256,512]{2,1,0:T(8,128)(2,1)S(1)}, f32[256,512]{1,0:T(8,128)S(1)}) custom-call(s32[2]{0:T(128)S(1)} %get-tuple-element.19.info_ref, s32[128,1]{1,0:T(8,128)S(1)} %copy.15.cols_ref, bf16[512,8192]{1,0:T(8,128)(2,1)S(1)} %copy-done.1, bf16[512,8192]{1,0:T(8,128)(2,1)S(1)} %copy-done.5), custom_call_target="tpu_custom_call" | custom-call | flops 1073741824 | bytes 8388608 | tf_op jit(solution)/shard_map/pallas_call | solution.py:120
  38.1 0.1 select_reduce_fusion.1
  38.2 0.0 collective-permute-done
  38.2 2.2 %add.119 = bf16[8,256,512]{2,1,0:T(8,128)(2,1)S(1)} add(bf16[8,256,512]{2,1,0:T(8,128)(2,1)S(1)} %get-tuple-element.8, bf16[8,256,512]{2,1,0:T(8,128)(2,1)} %collective-permute-done) | non-fusion elementwise | flops 1048576 | bytes 6291456 | tf_op jit(solution)/shard_map/add | solution.py:84
  40.5 0.2 fusion.10
  40.7 2.6 %collective-permute-start.1 = (bf16[2,2,128,512]{3,2,1,0:T(8,128)(2,1)S(1)}, bf16[2,2,128,512]{3,2,1,0:T(8,128)(2,1)S(1)}, u32[]{:S(2)}, u32[]{:S(2)}) collective-permute-start(bf16[2,2,128,512]{3,2,1,0:T(8,128)(2,1)S(1)} %dynamic-slice_bitcast_fusion.1), channel_id=1, source_target_pairs={{0,2},{1,3},{2,0},{3,1},{4,6},{5,7},{6,4},{7,5},{8,10},{9,11},{10,... | collective-permute-start | bytes 1572872 | tf_op jit(solution)/shard_map/ppermute | solution.py:73
  43.4 1.6 collective-permute-start.4
  45.0 10.9 %collective-permute-done.1 = bf16[2,2,128,512]{3,2,1,0:T(8,128)(2,1)S(1)} collective-permute-done((bf16[2,2,128,512]{3,2,1,0:T(8,128)(2,1)S(1)}, bf16[2,2,128,512]{3,2,1,0:T(8,128)(2,1)S(1)}, u32[]{:S(2)}, u32[]{:S(2)}) %collective-permute-start.1) | collective-permute-done | bytes 524320 | tf_op jit(solution)/shard_map/ppermute | solution.py:73
  55.9 0.1 bitcast_add_fusion.2
  56.0 1.9 %collective-permute-start.2 = (bf16[2,128,512]{2,1,0:T(8,128)(2,1)S(1)}, bf16[2,128,512]{2,1,0:T(8,128)(2,1)S(1)}, u32[]{:S(2)}, u32[]{:S(2)}) collective-permute-start(bf16[2,128,512]{2,1,0:T(8,128)(2,1)S(1)} %dynamic-slice_bitcast_fusion.3), channel_id=1, source_target_pairs={{0,4},{1,5},{2,6},{3,7},{4,0},{5,1},{6,2},{7,3},{8,12},{9,13},{10,... | collective-permute-start | bytes 786440 | tf_op jit(solution)/shard_map/ppermute | solution.py:73
  57.8 0.1 bitcast_add_fusion.5
  57.9 2.7 %collective-permute-start.5 = (bf16[2,128,512]{2,1,0:T(8,128)(2,1)S(1)}, bf16[2,128,512]{2,1,0:T(8,128)(2,1)S(1)}, u32[]{:S(2)}, u32[]{:S(2)}) collective-permute-start(bf16[2,128,512]{2,1,0:T(8,128)(2,1)S(1)} %dynamic-slice_bitcast_fusion.2), channel_id=1, source_target_pairs={{0,8},{1,9},{2,10},{3,11},{4,12},{5,13},{6,14},{7,15},{8,0},{9,1},... | collective-permute-start | bytes 786440 | tf_op jit(solution)/shard_map/ppermute | solution.py:73
  60.6 8.9 %collective-permute-done.2 = bf16[2,128,512]{2,1,0:T(8,128)(2,1)S(1)} collective-permute-done((bf16[2,128,512]{2,1,0:T(8,128)(2,1)S(1)}, bf16[2,128,512]{2,1,0:T(8,128)(2,1)S(1)}, u32[]{:S(2)}, u32[]{:S(2)}) %collective-permute-start.2) | collective-permute-done | bytes 262176 | tf_op jit(solution)/shard_map/ppermute | solution.py:73
  69.5 0.1 collective-permute-start.3
  69.6 5.6 %collective-permute-done.5 = bf16[2,128,512]{2,1,0:T(8,128)(2,1)S(1)} collective-permute-done((bf16[2,128,512]{2,1,0:T(8,128)(2,1)S(1)}, bf16[2,128,512]{2,1,0:T(8,128)(2,1)S(1)}, u32[]{:S(2)}, u32[]{:S(2)}) %collective-permute-start.5) | collective-permute-done | bytes 262176 | tf_op jit(solution)/shard_map/ppermute | solution.py:73
  75.2 1.6 collective-permute-start.6
  76.8 1.0 collective-permute-done.3
  77.8 2.5 %collective-permute-done.6 = bf16[128,512]{1,0:T(8,128)(2,1)S(1)} collective-permute-done((bf16[128,512]{1,0:T(8,128)(2,1)S(1)}, bf16[128,512]{1,0:T(8,128)(2,1)S(1)}, u32[]{:S(2)}, u32[]{:S(2)}) %collective-permute-start.6) | collective-permute-done | bytes 131104 | tf_op jit(solution)/shard_map/ppermute | solution.py:73
  80.3 0.9 divide_convert_fusion.panel_ref
  81.2 0.0 all-gather.3.cloned.1.call-update
  81.2 0.1 broadcast_in_dim.17
  81.3 0.1 reshape.49.scale_ref
  81.4 3.4 %copy-done.2 = bf16[512,8192]{1,0:T(8,128)(2,1)S(1)} copy-done((bf16[512,8192]{1,0:T(8,128)(2,1)S(1)}, bf16[512,8192]{1,0:T(8,128)(2,1)}, u32[]{:S(2)}) %copy-start.2) | copy-done | bytes 8388632
  84.8 3.4 %copy-done.6 = bf16[512,8192]{1,0:T(8,128)(2,1)S(1)} copy-done((bf16[512,8192]{1,0:T(8,128)(2,1)S(1)}, bf16[512,8192]{1,0:T(8,128)(2,1)}, u32[]{:S(2)}) %copy-start.6) | copy-done | bytes 8388632
  88.2 0.9 copy-done.8
  89.1 4.8 %shard_map.63 = bf16[8,256,512]{2,1,0:T(8,128)(2,1)S(1)} custom-call(s32[1]{0:T(128)} %bitcast.2.info_ref, f32[16]{0:T(128)S(1)} %reshape.49.scale_ref, bf16[256,512]{1,0:T(8,128)(2,1)S(1)} %copy-done.8, bf16[512,8192]{1,0:T(8,128)(2,1)S(1)} %copy-done.2, bf16[512,8192]{1,0:T(8,128)(2,1)S(1)} %copy-done.6), custom_call_target="tpu_custom_call" | custom-call | flops 1073741824 | bytes 8388608 | tf_op jit(solution)/shard_map/pallas_call | solution.py:137
  93.9 0.1 collective-permute-start.7
  94.0 4.8 %shard_map.62 = f32[8,256,512]{2,1,0:T(8,128)S(1)} custom-call(s32[1]{0:T(128)} %bitcast.5.info_ref, f32[16]{0:T(128)S(1)} %reshape.49.scale_ref, bf16[256,512]{1,0:T(8,128)(2,1)S(1)} %copy-done.9, bf16[512,8192]{1,0:T(8,128)(2,1)S(1)} %copy-done.2, bf16[512,8192]{1,0:T(8,128)(2,1)S(1)} %copy-done.6), custom_call_target="tpu_custom_call" | custom-call | flops 1073741824 | bytes 8388608 | tf_op jit(solution)/shard_map/pallas_call | solution.py:137
  98.8 0.0 collective-permute-done.7
  98.8 0.8 convert_add_fusion
  99.6 0.6 fusion.9
  100.2 0.1 fusion.1
  100.3 1.6 collective-permute-start.11
  101.9 0.1 fusion
  102.0 0.7 collective-permute-start.8
  102.7 19.5 %collective-permute-done.11 = bf16[2,2,128,512]{3,2,1,0:T(8,128)(2,1)S(1)} collective-permute-done((bf16[2,2,128,512]{3,2,1,0:T(8,128)(2,1)S(1)}, bf16[2,2,128,512]{3,2,1,0:T(8,128)(2,1)S(1)}, u32[]{:S(2)}, u32[]{:S(2)}) %collective-permute-start.11) | collective-permute-done | bytes 524320 | tf_op jit(solution)/shard_map/ppermute | solution.py:73
  122.3 0.2 bitcast_add_fusion
  122.5 4.3 %collective-permute-start.12 = (bf16[2,128,512]{2,1,0:T(8,128)(2,1)S(1)}, bf16[2,128,512]{2,1,0:T(8,128)(2,1)S(1)}, u32[]{:S(2)}, u32[]{:S(2)}) collective-permute-start(bf16[2,128,512]{2,1,0:T(8,128)(2,1)S(1)} %fusion.3), channel_id=1, source_target_pairs={{0,8},{1,9},{2,10},{3,11},{4,12},{5,13},{6,14},{7,15},{8,0},{9,1},... | collective-permute-start | bytes 786440 | tf_op jit(solution)/shard_map/ppermute | solution.py:73
  126.8 0.2 bitcast_add_fusion.1
  127.0 2.5 %collective-permute-start.9 = (bf16[2,128,512]{2,1,0:T(8,128)(2,1)S(1)}, bf16[2,128,512]{2,1,0:T(8,128)(2,1)S(1)}, u32[]{:S(2)}, u32[]{:S(2)}) collective-permute-start(bf16[2,128,512]{2,1,0:T(8,128)(2,1)S(1)} %fusion.2), channel_id=1, source_target_pairs={{0,4},{1,5},{2,6},{3,7},{4,0},{5,1},{6,2},{7,3},{8,12},{9,13},{10,... | collective-permute-start | bytes 786440 | tf_op jit(solution)/shard_map/ppermute | solution.py:73
  129.6 16.3 %collective-permute-done.12 = bf16[2,128,512]{2,1,0:T(8,128)(2,1)S(1)} collective-permute-done((bf16[2,128,512]{2,1,0:T(8,128)(2,1)S(1)}, bf16[2,128,512]{2,1,0:T(8,128)(2,1)S(1)}, u32[]{:S(2)}, u32[]{:S(2)}) %collective-permute-start.12) | collective-permute-done | bytes 262176 | tf_op jit(solution)/shard_map/ppermute | solution.py:73
  145.9 0.1 bitcast_add_fusion.3
  146.0 0.1 collective-permute-start.13
  146.1 0.1 bitcast_add_fusion.4
  146.2 1.9 %collective-permute-start.10 = (bf16[128,512]{1,0:T(8,128)(2,1)S(1)}, bf16[128,512]{1,0:T(8,128)(2,1)S(1)}, u32[]{:S(2)}, u32[]{:S(2)}) collective-permute-start(bf16[128,512]{1,0:T(8,128)(2,1)S(1)} %fusion.4), channel_id=1, source_target_pairs={{0,8},{1,9},{2,10},{3,11},{4,12},{5,13},{6,14},{7,15},{8,0},{9,1},... | collective-permute-start | bytes 393224 | tf_op jit(solution)/shard_map/ppermute | solution.py:73
  148.1 3.0 %collective-permute-done.13 = bf16[128,512]{1,0:T(8,128)(2,1)S(1)} collective-permute-done((bf16[128,512]{1,0:T(8,128)(2,1)S(1)}, bf16[128,512]{1,0:T(8,128)(2,1)S(1)}, u32[]{:S(2)}, u32[]{:S(2)}) %collective-permute-start.13) | collective-permute-done | bytes 131104 | tf_op jit(solution)/shard_map/ppermute | solution.py:73
  151.1 3.6 %collective-permute-done.10 = bf16[128,512]{1,0:T(8,128)(2,1)S(1)} collective-permute-done((bf16[128,512]{1,0:T(8,128)(2,1)S(1)}, bf16[128,512]{1,0:T(8,128)(2,1)S(1)}, u32[]{:S(2)}, u32[]{:S(2)}) %collective-permute-start.10) | collective-permute-done | bytes 131104 | tf_op jit(solution)/shard_map/ppermute | solution.py:73
  154.7 0.0 all-gather.3.cloned.1.call-done
  154.7 0.0 copy-start.3
  154.8 3.4 %copy-done.3 = bf16[512,8192]{1,0:T(8,128)(2,1)S(1)} copy-done((bf16[512,8192]{1,0:T(8,128)(2,1)S(1)}, bf16[512,8192]{1,0:T(8,128)(2,1)}, u32[]{:S(2)}) %copy-start.3) | copy-done | bytes 8388632
  158.1 3.4 %copy-done.7 = bf16[512,8192]{1,0:T(8,128)(2,1)S(1)} copy-done((bf16[512,8192]{1,0:T(8,128)(2,1)S(1)}, bf16[512,8192]{1,0:T(8,128)(2,1)}, u32[]{:S(2)}) %copy-start.7) | copy-done | bytes 8388632
  161.5 2.2 %copy-done.10 = bf16[4096,512]{1,0:T(8,128)(2,1)S(1)} copy-done((bf16[4096,512]{1,0:T(8,128)(2,1)S(1)}, bf16[4096,512]{1,0:T(8,128)(2,1)}, u32[]{:S(2)}) %copy-start.10) | copy-done | bytes 4194328
  163.7 9.8 %shard_map.61.front_ref = f32[512,256]{1,0:T(8,128)S(1)} custom-call(f32[16]{0:T(128)S(1)} %reshape.49.scale_ref, bf16[16,256,512]{2,1,0:T(8,128)(2,1)S(1)} %bitcast.74, bf16[512,8192]{1,0:T(8,128)(2,1)S(1)} %copy-done.3, bf16[512,8192]{1,0:T(8,128)(2,1)S(1)} %copy-done.7), custom_call_target="tpu_custom_call" | custom-call | flops 2147483648 | bytes 16777216 | tf_op jit(solution)/shard_map/pallas_call | solution.py:164
  173.5 0.9 shard_map.64
  (39 shorter events, 0.5 us)
Async XLA Ops:
  7.2 147.6 %all-gather.3.cloned.1.call-start = ((), (), s32[]{:S(2)}) async-start(), calls=%async_computation | async-start | bytes 4456448 | tf_op jit(solution)/shard_map/all_gather | solution.py:159
  8.1 3.4 %copy-start = (bf16[512,8192]{1,0:T(8,128)(2,1)S(1)}, bf16[512,8192]{1,0:T(8,128)(2,1)}, u32[]{:S(2)}) copy-start(bf16[512,8192]{1,0:T(8,128)(2,1)} %dr_ref.9) | copy-start | bytes 25165828
  11.4 3.4 %copy-start.4 = (bf16[512,8192]{1,0:T(8,128)(2,1)S(1)}, bf16[512,8192]{1,0:T(8,128)(2,1)}, u32[]{:S(2)}) copy-start(bf16[512,8192]{1,0:T(8,128)(2,1)} %di_ref.9) | copy-start | bytes 25165828
  14.8 8.4 %copy-start.11 = (s32[8,8]{1,0:T(8,128)S(1)}, s32[8,8]{1,0:T(8,128)}, u32[]{:S(2)}) copy-start(s32[8,8]{1,0:T(8,128)} %param.6) | copy-start | bytes 772
  22.7 15.5 %collective-permute-start = (bf16[8,256,512]{2,1,0:T(8,128)(2,1)S(1)}, bf16[8,256,512]{2,1,0:T(8,128)(2,1)}, u32[]{:S(2)}, u32[]{:S(2)}) collective-permute-start(bf16[8,256,512]{2,1,0:T(8,128)(2,1)S(1)} %get-tuple-element.9), channel_id=1, source_target_pairs={{0,1},{1,0},{2,3},{3,2},{4,5},{5,4},{6,7},{7,6},{8,9},{9,8},{10,11... | collective-permute-start | bytes 6291464 | tf_op jit(solution)/shard_map/ppermute | solution.py:73
  23.4 3.4 %copy-start.1 = (bf16[512,8192]{1,0:T(8,128)(2,1)S(1)}, bf16[512,8192]{1,0:T(8,128)(2,1)}, u32[]{:S(2)}) copy-start(bf16[512,8192]{1,0:T(8,128)(2,1)} %dr_ref.9) | copy-start | bytes 25165828
  26.8 3.4 %copy-start.5 = (bf16[512,8192]{1,0:T(8,128)(2,1)S(1)}, bf16[512,8192]{1,0:T(8,128)(2,1)}, u32[]{:S(2)}) copy-start(bf16[512,8192]{1,0:T(8,128)(2,1)} %di_ref.9) | copy-start | bytes 25165828
  30.2 7.9 %copy-start.12 = (s32[128]{0:T(128)S(1)}, s32[128]{0:T(128)}, u32[]{:S(2)}) copy-start(s32[128]{0:T(128)} %param.7) | copy-start | bytes 1540
  40.7 15.2 %collective-permute-start.1 = (bf16[2,2,128,512]{3,2,1,0:T(8,128)(2,1)S(1)}, bf16[2,2,128,512]{3,2,1,0:T(8,128)(2,1)S(1)}, u32[]{:S(2)}, u32[]{:S(2)}) collective-permute-start(bf16[2,2,128,512]{3,2,1,0:T(8,128)(2,1)S(1)} %dynamic-slice_bitcast_fusion.1), channel_id=1, source_target_pairs={{0,2},{1,3},{2,0},{3,1},{4,6},{5,7},{6,4},{7,5},{8,10},{9,11},{10,... | collective-permute-start | bytes 1572872 | tf_op jit(solution)/shard_map/ppermute | solution.py:73
  43.4 14.5 %collective-permute-start.4 = (bf16[2,2,128,512]{3,2,1,0:T(8,128)(2,1)S(1)}, bf16[2,2,128,512]{3,2,1,0:T(8,128)(2,1)S(1)}, u32[]{:S(2)}, u32[]{:S(2)}) collective-permute-start(bf16[2,2,128,512]{3,2,1,0:T(8,128)(2,1)S(1)} %dynamic-slice_bitcast_fusion), channel_id=1, source_target_pairs={{0,4},{1,5},{2,6},{3,7},{4,0},{5,1},{6,2},{7,3},{8,12},{9,13},{10,... | collective-permute-start | bytes 1572872 | tf_op jit(solution)/shard_map/ppermute | solution.py:73
  56.0 13.5 %collective-permute-start.2 = (bf16[2,128,512]{2,1,0:T(8,128)(2,1)S(1)}, bf16[2,128,512]{2,1,0:T(8,128)(2,1)S(1)}, u32[]{:S(2)}, u32[]{:S(2)}) collective-permute-start(bf16[2,128,512]{2,1,0:T(8,128)(2,1)S(1)} %dynamic-slice_bitcast_fusion.3), channel_id=1, source_target_pairs={{0,4},{1,5},{2,6},{3,7},{4,0},{5,1},{6,2},{7,3},{8,12},{9,13},{10,... | collective-permute-start | bytes 786440 | tf_op jit(solution)/shard_map/ppermute | solution.py:73
  57.9 17.2 %collective-permute-start.5 = (bf16[2,128,512]{2,1,0:T(8,128)(2,1)S(1)}, bf16[2,128,512]{2,1,0:T(8,128)(2,1)S(1)}, u32[]{:S(2)}, u32[]{:S(2)}) collective-permute-start(bf16[2,128,512]{2,1,0:T(8,128)(2,1)S(1)} %dynamic-slice_bitcast_fusion.2), channel_id=1, source_target_pairs={{0,8},{1,9},{2,10},{3,11},{4,12},{5,13},{6,14},{7,15},{8,0},{9,1},... | collective-permute-start | bytes 786440 | tf_op jit(solution)/shard_map/ppermute | solution.py:73
  69.5 8.3 %collective-permute-start.3 = (bf16[128,512]{1,0:T(8,128)(2,1)S(1)}, bf16[128,512]{1,0:T(8,128)(2,1)S(1)}, u32[]{:S(2)}, u32[]{:S(2)}) collective-permute-start(bf16[128,512]{1,0:T(8,128)(2,1)S(1)} %dynamic-slice_bitcast_fusion.5), channel_id=1, source_target_pairs={{0,8},{1,9},{2,10},{3,11},{4,12},{5,13},{6,14},{7,15},{8,0},{9,1},... | collective-permute-start | bytes 393224 | tf_op jit(solution)/shard_map/ppermute | solution.py:73
  75.2 5.0 %collective-permute-start.6 = (bf16[128,512]{1,0:T(8,128)(2,1)S(1)}, bf16[128,512]{1,0:T(8,128)(2,1)S(1)}, u32[]{:S(2)}, u32[]{:S(2)}) collective-permute-start(bf16[128,512]{1,0:T(8,128)(2,1)S(1)} %dynamic-slice_bitcast_fusion.4), channel_id=1, source_target_pairs={{0,2},{1,3},{2,0},{3,1},{4,6},{5,7},{6,4},{7,5},{8,10},{9,11},{10,... | collective-permute-start | bytes 393224 | tf_op jit(solution)/shard_map/ppermute | solution.py:73
  81.4 3.4 %copy-start.2 = (bf16[512,8192]{1,0:T(8,128)(2,1)S(1)}, bf16[512,8192]{1,0:T(8,128)(2,1)}, u32[]{:S(2)}) copy-start(bf16[512,8192]{1,0:T(8,128)(2,1)} %dr_ref.9) | copy-start | bytes 25165828
  84.8 3.4 %copy-start.6 = (bf16[512,8192]{1,0:T(8,128)(2,1)S(1)}, bf16[512,8192]{1,0:T(8,128)(2,1)}, u32[]{:S(2)}) copy-start(bf16[512,8192]{1,0:T(8,128)(2,1)} %di_ref.9) | copy-start | bytes 25165828
  88.2 0.9 copy-start.8
  89.1 4.9 %copy-start.9 = (bf16[256,512]{1,0:T(8,128)(2,1)S(1)}, bf16[256,512]{1,0:T(8,128)(2,1)}, u32[]{:S(2)}) copy-start(bf16[256,512]{1,0:T(8,128)(2,1)} %divide_convert_fusion.panel_ref) | copy-start | bytes 786436
  93.9 4.9 %collective-permute-start.7 = (bf16[8,256,512]{2,1,0:T(8,128)(2,1)S(1)}, bf16[8,256,512]{2,1,0:T(8,128)(2,1)S(1)}, u32[]{:S(2)}, u32[]{:S(2)}) collective-permute-start(bf16[8,256,512]{2,1,0:T(8,128)(2,1)S(1)} %shard_map.63), channel_id=1, source_target_pairs={{0,1},{1,0},{2,3},{3,2},{4,5},{5,4},{6,7},{7,6},{8,9},{9,8},{10,11... | collective-permute-start | bytes 6291464 | tf_op jit(solution)/shard_map/ppermute | solution.py:73
  100.3 21.9 %collective-permute-start.11 = (bf16[2,2,128,512]{3,2,1,0:T(8,128)(2,1)S(1)}, bf16[2,2,128,512]{3,2,1,0:T(8,128)(2,1)S(1)}, u32[]{:S(2)}, u32[]{:S(2)}) collective-permute-start(bf16[2,2,128,512]{3,2,1,0:T(8,128)(2,1)S(1)} %fusion.1), channel_id=1, source_target_pairs={{0,4},{1,5},{2,6},{3,7},{4,0},{5,1},{6,2},{7,3},{8,12},{9,13},{10,... | collective-permute-start | bytes 1572872 | tf_op jit(solution)/shard_map/ppermute | solution.py:73
  102.0 24.8 %collective-permute-start.8 = (bf16[2,2,128,512]{3,2,0,1:T(8,128)(2,1)S(1)}, bf16[2,2,128,512]{3,2,0,1:T(8,128)(2,1)S(1)}, u32[]{:S(2)}, u32[]{:S(2)}) collective-permute-start(bf16[2,2,128,512]{3,2,0,1:T(8,128)(2,1)S(1)} %fusion), channel_id=1, source_target_pairs={{0,2},{1,3},{2,0},{3,1},{4,6},{5,7},{6,4},{7,5},{8,10},{9,11},{10,... | collective-permute-start | bytes 1572872 | tf_op jit(solution)/shard_map/ppermute | solution.py:73
  122.5 23.4 %collective-permute-start.12 = (bf16[2,128,512]{2,1,0:T(8,128)(2,1)S(1)}, bf16[2,128,512]{2,1,0:T(8,128)(2,1)S(1)}, u32[]{:S(2)}, u32[]{:S(2)}) collective-permute-start(bf16[2,128,512]{2,1,0:T(8,128)(2,1)S(1)} %fusion.3), channel_id=1, source_target_pairs={{0,8},{1,9},{2,10},{3,11},{4,12},{5,13},{6,14},{7,15},{8,0},{9,1},... | collective-permute-start | bytes 786440 | tf_op jit(solution)/shard_map/ppermute | solution.py:73
  127.0 19.1 %collective-permute-start.9 = (bf16[2,128,512]{2,1,0:T(8,128)(2,1)S(1)}, bf16[2,128,512]{2,1,0:T(8,128)(2,1)S(1)}, u32[]{:S(2)}, u32[]{:S(2)}) collective-permute-start(bf16[2,128,512]{2,1,0:T(8,128)(2,1)S(1)} %fusion.2), channel_id=1, source_target_pairs={{0,4},{1,5},{2,6},{3,7},{4,0},{5,1},{6,2},{7,3},{8,12},{9,13},{10,... | collective-permute-start | bytes 786440 | tf_op jit(solution)/shard_map/ppermute | solution.py:73
  146.0 5.0 %collective-permute-start.13 = (bf16[128,512]{1,0:T(8,128)(2,1)S(1)}, bf16[128,512]{1,0:T(8,128)(2,1)S(1)}, u32[]{:S(2)}, u32[]{:S(2)}) collective-permute-start(bf16[128,512]{1,0:T(8,128)(2,1)S(1)} %fusion.5), channel_id=1, source_target_pairs={{0,2},{1,3},{2,0},{3,1},{4,6},{5,7},{6,4},{7,5},{8,10},{9,11},{10,... | collective-permute-start | bytes 393224 | tf_op jit(solution)/shard_map/ppermute | solution.py:73
  146.2 8.5 %collective-permute-start.10 = (bf16[128,512]{1,0:T(8,128)(2,1)S(1)}, bf16[128,512]{1,0:T(8,128)(2,1)S(1)}, u32[]{:S(2)}, u32[]{:S(2)}) collective-permute-start(bf16[128,512]{1,0:T(8,128)(2,1)S(1)} %fusion.4), channel_id=1, source_target_pairs={{0,8},{1,9},{2,10},{3,11},{4,12},{5,13},{6,14},{7,15},{8,0},{9,1},... | collective-permute-start | bytes 393224 | tf_op jit(solution)/shard_map/ppermute | solution.py:73
  154.7 3.4 %copy-start.3 = (bf16[512,8192]{1,0:T(8,128)(2,1)S(1)}, bf16[512,8192]{1,0:T(8,128)(2,1)}, u32[]{:S(2)}) copy-start(bf16[512,8192]{1,0:T(8,128)(2,1)} %dr_ref.9) | copy-start | bytes 25165828
  158.1 3.4 %copy-start.7 = (bf16[512,8192]{1,0:T(8,128)(2,1)S(1)}, bf16[512,8192]{1,0:T(8,128)(2,1)}, u32[]{:S(2)}) copy-start(bf16[512,8192]{1,0:T(8,128)(2,1)} %di_ref.9) | copy-start | bytes 25165828
  161.5 2.2 %copy-start.10 = (bf16[4096,512]{1,0:T(8,128)(2,1)S(1)}, bf16[4096,512]{1,0:T(8,128)(2,1)}, u32[]{:S(2)}) copy-start(bf16[4096,512]{1,0:T(8,128)(2,1)} %all-gather.3.cloned.1.call-done) | copy-start | bytes 12582916
Sparse Core Ops, SparseCore 0:
  81.4 65.5 all-gather.2

commit v3 on v2

--- a/solution.py
+++ b/solution.py
@@ -109,6 +109,7 @@
     scale = jnp.repeat(forward / denom, n // TILES)
     smem = pl.BlockSpec(memory_space=pltpu.SMEM)
     params = pltpu.CompilerParams(vmem_limit_bytes=32 << 20)
+    large = pltpu.CompilerParams(vmem_limit_bytes=50 << 20)
     cost = pl.CostEstimate(flops=2 * rows * width * pair, bytes_accessed=4 * rows * width, transcendentals=0)
     half_cost = pl.CostEstimate(flops=rows * width * pair, bytes_accessed=2 * rows * width, transcendentals=0)
     whole = lambda shape: pl.BlockSpec(shape, lambda j, *refs: (0,) * len(shape))
@@ -129,7 +130,7 @@
                 jax.ShapeDtypeStruct((n // 2, pair, rows), jnp.bfloat16),
                 jax.ShapeDtypeStruct((pair, rows), jnp.float32),
             ),
-            compiler_params=params,
+            compiler_params=large,
             cost_estimate=half_cost,
         )(jnp.stack([target, row0]), cols, data_real, data_imag)
 
@@ -143,7 +144,7 @@
                 out_specs=stacked,
             ),
             out_shape=jax.ShapeDtypeStruct((n // 2, pair, rows), kind),
-            compiler_params=params,
+            compiler_params=large,
             cost_estimate=half_cost,
         )(target.reshape(1), scale, panel, data_real, data_imag)
 
@@ -172,7 +173,7 @@
             pl.BlockSpec((rows, rows), lambda j: (0, j)),
         ],
         out_specs=whole((rows, pair)),
-        compiler_params=params,
+        compiler_params=large,
         cost_estimate=cost,
     )(scale, panels, data_real, data_imag)
     return pl.pallas_call(

time: 182 us -> 171 us (0.940)
  local copies, waits for them, and re-layouts: 32.5 us -> 3.19 us
  Pallas kernels: 36.1 us -> 52.3 us
  other arithmetic: 4.9 us -> 7.03 us
    unnamed x26 -> x8, local copies, waits for them, and re-layouts: 30.2 us -> 0.96 us
    pallas_call x2, Pallas kernels: 9.59 us -> 16.4 us  [back(): pl.pallas_call(back_kernel, grid_spec=pltpu.PrefetchScalarGridSpec(num_sc...]
    pallas_call x1, Pallas kernels: 9.8 us -> 15.4 us  [shards(): pl.pallas_call(front_kernel, grid=(n,), out_shape=jax.ShapeDtypeStruct((r...]
    pallas_call x2, Pallas kernels: 15.8 us -> 19.6 us  [pick(): pl.pallas_call(pick_kernel, grid_spec=pltpu.PrefetchScalarGridSpec(num_sc...]
    add x2, other arithmetic: 3.05 us -> 5.16 us  [scattered(): total = kept + got.astype(kept.dtype)]
  transfers between devices with their start and end apart: 15 -> 15, of which waited for: 9 -> 9; matrix products, arithmetic and copies ran while one was open for 2% -> 3% of each run, Pallas kernels for 10% -> 15%
where the time goes in v3:
time: 171 us; the launch traced here: 170 us
  waiting for transfers between devices  70.8 us (41%)
  Pallas kernels  52.3 us (31%)
  starting transfers between devices  22.2 us (13%)
  between operations  14.3 us (8%)
  other arithmetic  7.03 us (4%)
  local copies, waits for them, and re-layouts  3.19 us (2%)
    ppermute x14, waiting for transfers between devices, swap(): return lax.ppermute(x, 'row', [(i, i ^ 1 << bit) for i in range(n)])  70.8 us
    ppermute x14, starting transfers between devices, swap(): return lax.ppermute(x, 'row', [(i, i ^ 1 << bit) for i in range(n)])  22.2 us
    pallas_call x2, Pallas kernels, pick(): pl.pallas_call(pick_kernel, grid_spec=pltpu.PrefetchScalarGridSpec(num_sc...  19.6 us
    pallas_call x2, Pallas kernels, back(): pl.pallas_call(back_kernel, grid_spec=pltpu.PrefetchScalarGridSpec(num_sc...  16.4 us
    pallas_call x1, Pallas kernels, shards(): pl.pallas_call(front_kernel, grid=(n,), out_shape=jax.ShapeDtypeStruct((r...  15.4 us
    add x2, other arithmetic, scattered(): total = kept + got.astype(kept.dtype)  5.16 us
  transfers between devices with their start and end apart: 15, of which 9 were waited for; matrix products, arithmetic and copies ran while one was open for 3% of the time, Pallas kernels for 15%

profile of v3, /device:TPU:0, one launch (start us, length us, event | category | flops | bytes accessed | tf_op | source)
XLA Modules:
  0.0 169.8 jit_solution(13281577289051232159)
XLA Ops:
  7.2 0.0 all-gather.3.cloned.1.call-start
  7.2 0.8 copy.15.cols_ref
  8.0 0.1 pad_add_fusion
  8.1 0.0 copy-start.2
  8.1 9.8 %shard_map.59 = (bf16[8,256,512]{2,1,0:T(8,128)(2,1)S(1)}, f32[256,512]{1,0:T(8,128)S(1)}) custom-call(s32[2]{0:T(128)S(1)} %get-tuple-element.18.info_ref, s32[128,1]{1,0:T(8,128)S(1)} %copy.15.cols_ref, bf16[512,8192]{1,0:T(8,128)(2,1)} %dr_ref.9, bf16[512,8192]{1,0:T(8,128)(2,1)} %di_ref.9), custom_call_target="tpu_custom_call" | custom-call | flops 1073741824 | bytes 8388608 | tf_op jit(solution)/shard_map/pallas_call | solution.py:121
  17.8 0.5 collective-permute-start
  18.4 0.0 copy-done.2
  18.4 0.2 fusion.6
  18.6 0.0 copy-start.3
  18.6 9.8 %shard_map.60 = (bf16[8,256,512]{2,1,0:T(8,128)(2,1)S(1)}, f32[256,512]{1,0:T(8,128)S(1)}) custom-call(s32[2]{0:T(128)S(1)} %get-tuple-element.19.info_ref, s32[128,1]{1,0:T(8,128)S(1)} %copy.15.cols_ref, bf16[512,8192]{1,0:T(8,128)(2,1)} %dr_ref.9, bf16[512,8192]{1,0:T(8,128)(2,1)} %di_ref.9), custom_call_target="tpu_custom_call" | custom-call | flops 1073741824 | bytes 8388608 | tf_op jit(solution)/shard_map/pallas_call | solution.py:121
  28.4 0.0 copy-done.3
  28.4 0.1 select_reduce_fusion.1
  28.5 0.0 collective-permute-done
  28.5 2.2 %add.119 = bf16[8,256,512]{2,1,0:T(8,128)(2,1)S(1)} add(bf16[8,256,512]{2,1,0:T(8,128)(2,1)S(1)} %get-tuple-element.8, bf16[8,256,512]{2,1,0:T(8,128)(2,1)} %collective-permute-done) | non-fusion elementwise | flops 1048576 | bytes 6291456 | tf_op jit(solution)/shard_map/add | solution.py:84
  30.7 0.2 fusion.10
  31.0 2.6 %collective-permute-start.1 = (bf16[2,2,128,512]{3,2,1,0:T(8,128)(2,1)S(1)}, bf16[2,2,128,512]{3,2,1,0:T(8,128)(2,1)S(1)}, u32[]{:S(2)}, u32[]{:S(2)}) collective-permute-start(bf16[2,2,128,512]{3,2,1,0:T(8,128)(2,1)S(1)} %dynamic-slice_bitcast_fusion.1), channel_id=1, source_target_pairs={{0,2},{1,3},{2,0},{3,1},{4,6},{5,7},{6,4},{7,5},{8,10},{9,11},{10,... | collective-permute-start | bytes 1572872 | tf_op jit(solution)/shard_map/ppermute | solution.py:73
  33.7 1.6 collective-permute-start.4
  35.3 10.9 %collective-permute-done.1 = bf16[2,2,128,512]{3,2,1,0:T(8,128)(2,1)S(1)} collective-permute-done((bf16[2,2,128,512]{3,2,1,0:T(8,128)(2,1)S(1)}, bf16[2,2,128,512]{3,2,1,0:T(8,128)(2,1)S(1)}, u32[]{:S(2)}, u32[]{:S(2)}) %collective-permute-start.1) | collective-permute-done | bytes 524320 | tf_op jit(solution)/shard_map/ppermute | solution.py:73
  46.2 0.1 bitcast_add_fusion.2
  46.2 1.9 %collective-permute-start.2 = (bf16[2,128,512]{2,1,0:T(8,128)(2,1)S(1)}, bf16[2,128,512]{2,1,0:T(8,128)(2,1)S(1)}, u32[]{:S(2)}, u32[]{:S(2)}) collective-permute-start(bf16[2,128,512]{2,1,0:T(8,128)(2,1)S(1)} %dynamic-slice_bitcast_fusion.3), channel_id=1, source_target_pairs={{0,4},{1,5},{2,6},{3,7},{4,0},{5,1},{6,2},{7,3},{8,12},{9,13},{10,... | collective-permute-start | bytes 786440 | tf_op jit(solution)/shard_map/ppermute | solution.py:73
  48.1 0.0 collective-permute-done.4
  48.1 0.1 bitcast_add_fusion.5
  48.2 2.6 %collective-permute-start.5 = (bf16[2,128,512]{2,1,0:T(8,128)(2,1)S(1)}, bf16[2,128,512]{2,1,0:T(8,128)(2,1)S(1)}, u32[]{:S(2)}, u32[]{:S(2)}) collective-permute-start(bf16[2,128,512]{2,1,0:T(8,128)(2,1)S(1)} %dynamic-slice_bitcast_fusion.2), channel_id=1, source_target_pairs={{0,8},{1,9},{2,10},{3,11},{4,12},{5,13},{6,14},{7,15},{8,0},{9,1},... | collective-permute-start | bytes 786440 | tf_op jit(solution)/shard_map/ppermute | solution.py:73
  50.9 8.9 %collective-permute-done.2 = bf16[2,128,512]{2,1,0:T(8,128)(2,1)S(1)} collective-permute-done((bf16[2,128,512]{2,1,0:T(8,128)(2,1)S(1)}, bf16[2,128,512]{2,1,0:T(8,128)(2,1)S(1)}, u32[]{:S(2)}, u32[]{:S(2)}) %collective-permute-start.2) | collective-permute-done | bytes 262176 | tf_op jit(solution)/shard_map/ppermute | solution.py:73
  59.8 0.1 collective-permute-start.3
  59.9 5.6 %collective-permute-done.5 = bf16[2,128,512]{2,1,0:T(8,128)(2,1)S(1)} collective-permute-done((bf16[2,128,512]{2,1,0:T(8,128)(2,1)S(1)}, bf16[2,128,512]{2,1,0:T(8,128)(2,1)S(1)}, u32[]{:S(2)}, u32[]{:S(2)}) %collective-permute-start.5) | collective-permute-done | bytes 262176 | tf_op jit(solution)/shard_map/ppermute | solution.py:73
  65.5 1.6 collective-permute-start.6
  67.1 1.0 collective-permute-done.3
  68.1 2.5 %collective-permute-done.6 = bf16[128,512]{1,0:T(8,128)(2,1)S(1)} collective-permute-done((bf16[128,512]{1,0:T(8,128)(2,1)S(1)}, bf16[128,512]{1,0:T(8,128)(2,1)S(1)}, u32[]{:S(2)}, u32[]{:S(2)}) %collective-permute-start.6) | collective-permute-done | bytes 131104 | tf_op jit(solution)/shard_map/ppermute | solution.py:73
  70.6 0.9 divide_convert_fusion.panel_ref
  71.5 0.0 all-gather.3.cloned.1.call-update
  71.5 0.1 broadcast_in_dim.17
  71.6 0.1 reshape.49.scale_ref
  71.7 0.0 copy-start
  71.7 1.0 copy-done
  72.6 0.0 copy-start.1
  72.6 7.4 %shard_map.63 = bf16[8,256,512]{2,1,0:T(8,128)(2,1)S(1)} custom-call(s32[1]{0:T(128)} %bitcast.2.info_ref, f32[16]{0:T(128)S(1)} %reshape.49.scale_ref, bf16[256,512]{1,0:T(8,128)(2,1)S(1)} %copy-done, bf16[512,8192]{1,0:T(8,128)(2,1)} %dr_ref.9, bf16[512,8192]{1,0:T(8,128)(2,1)} %di_ref.9), custom_call_target="tpu_custom_call" | custom-call | flops 1073741824 | bytes 8388608 | tf_op jit(solution)/shard_map/pallas_call | solution.py:138
  80.0 0.1 collective-permute-start.7
  80.1 0.0 copy-done.1
  80.1 9.0 %shard_map.62 = f32[8,256,512]{2,1,0:T(8,128)} custom-call(s32[1]{0:T(128)} %bitcast.5.info_ref, f32[16]{0:T(128)S(1)} %reshape.49.scale_ref, bf16[256,512]{1,0:T(8,128)(2,1)S(1)} %copy-done.1, bf16[512,8192]{1,0:T(8,128)(2,1)} %dr_ref.9, bf16[512,8192]{1,0:T(8,128)(2,1)} %di_ref.9), custom_call_target="tpu_custom_call" | custom-call | flops 1073741824 | bytes 8388608 | tf_op jit(solution)/shard_map/pallas_call | solution.py:138
  89.1 0.0 collective-permute-done.7
  89.1 2.9 %convert_add_fusion = f32[8,256,512]{2,1,0:T(8,128)S(1)} fusion(f32[8,256,512]{2,1,0:T(8,128)} %shard_map.62, bf16[8,256,512]{2,1,0:T(8,128)(2,1)S(1)} %collective-permute-done.7), kind=kLoop, calls=%fused_computation | loop fusion | flops 2097152 | bytes 10485760 | tf_op jit(solution)/shard_map/add | solution.py:84
  92.0 0.5 fusion.9
  92.5 0.1 fusion.1
  92.6 1.6 collective-permute-start.11
  94.2 0.1 fusion
  94.3 0.9 collective-permute-start.8
  95.2 20.2 %collective-permute-done.11 = bf16[2,2,128,512]{3,2,1,0:T(8,128)(2,1)S(1)} collective-permute-done((bf16[2,2,128,512]{3,2,1,0:T(8,128)(2,1)S(1)}, bf16[2,2,128,512]{3,2,1,0:T(8,128)(2,1)S(1)}, u32[]{:S(2)}, u32[]{:S(2)}) %collective-permute-start.11) | collective-permute-done | bytes 524320 | tf_op jit(solution)/shard_map/ppermute | solution.py:73
  115.4 0.2 bitcast_add_fusion
  115.6 4.0 %collective-permute-start.12 = (bf16[2,128,512]{2,1,0:T(8,128)(2,1)S(1)}, bf16[2,128,512]{2,1,0:T(8,128)(2,1)S(1)}, u32[]{:S(2)}, u32[]{:S(2)}) collective-permute-start(bf16[2,128,512]{2,1,0:T(8,128)(2,1)S(1)} %fusion.3), channel_id=1, source_target_pairs={{0,8},{1,9},{2,10},{3,11},{4,12},{5,13},{6,14},{7,15},{8,0},{9,1},... | collective-permute-start | bytes 786440 | tf_op jit(solution)/shard_map/ppermute | solution.py:73
  119.6 0.0 collective-permute-done.8
  119.6 0.2 bitcast_add_fusion.1
  119.9 2.8 %collective-permute-start.9 = (bf16[2,128,512]{2,1,0:T(8,128)(2,1)S(1)}, bf16[2,128,512]{2,1,0:T(8,128)(2,1)S(1)}, u32[]{:S(2)}, u32[]{:S(2)}) collective-permute-start(bf16[2,128,512]{2,1,0:T(8,128)(2,1)S(1)} %fusion.2), channel_id=1, source_target_pairs={{0,4},{1,5},{2,6},{3,7},{4,0},{5,1},{6,2},{7,3},{8,12},{9,13},{10,... | collective-permute-start | bytes 786440 | tf_op jit(solution)/shard_map/ppermute | solution.py:73
  122.7 15.6 %collective-permute-done.12 = bf16[2,128,512]{2,1,0:T(8,128)(2,1)S(1)} collective-permute-done((bf16[2,128,512]{2,1,0:T(8,128)(2,1)S(1)}, bf16[2,128,512]{2,1,0:T(8,128)(2,1)S(1)}, u32[]{:S(2)}, u32[]{:S(2)}) %collective-permute-start.12) | collective-permute-done | bytes 262176 | tf_op jit(solution)/shard_map/ppermute | solution.py:73
  138.3 0.1 bitcast_add_fusion.3
  138.4 0.8 collective-permute-start.13
  139.2 0.0 collective-permute-done.9
  139.2 0.1 bitcast_add_fusion.4
  139.3 1.0 collective-permute-start.10
  140.3 3.1 %collective-permute-done.13 = bf16[128,512]{1,0:T(8,128)(2,1)S(1)} collective-permute-done((bf16[128,512]{1,0:T(8,128)(2,1)S(1)}, bf16[128,512]{1,0:T(8,128)(2,1)S(1)}, u32[]{:S(2)}, u32[]{:S(2)}) %collective-permute-start.13) | collective-permute-done | bytes 131104 | tf_op jit(solution)/shard_map/ppermute | solution.py:73
  143.5 3.0 %collective-permute-done.10 = bf16[128,512]{1,0:T(8,128)(2,1)S(1)} collective-permute-done((bf16[128,512]{1,0:T(8,128)(2,1)S(1)}, bf16[128,512]{1,0:T(8,128)(2,1)S(1)}, u32[]{:S(2)}, u32[]{:S(2)}) %collective-permute-start.10) | collective-permute-done | bytes 131104 | tf_op jit(solution)/shard_map/ppermute | solution.py:73
  146.6 0.0 all-gather.3.cloned.1.call-done
  146.6 15.4 %shard_map.61.front_ref = f32[512,256]{1,0:T(8,128)S(1)} custom-call(f32[16]{0:T(128)S(1)} %reshape.49.scale_ref, bf16[16,256,512]{2,1,0:T(8,128)(2,1)} %bitcast.82, bf16[512,8192]{1,0:T(8,128)(2,1)} %dr_ref.9, bf16[512,8192]{1,0:T(8,128)(2,1)} %di_ref.9), custom_call_target="tpu_custom_call" | custom-call | flops 2147483648 | bytes 16777216 | tf_op jit(solution)/shard_map/pallas_call | solution.py:165
  162.0 0.9 shard_map.64
  (21 shorter events, 0.5 us)
Async XLA Ops:
  7.2 139.4 %all-gather.3.cloned.1.call-start = ((), (), s32[]{:S(2)}) async-start(), calls=%async_computation | async-start | bytes 4456448 | tf_op jit(solution)/shard_map/all_gather | solution.py:160
  8.1 10.3 %copy-start.2 = (s32[8,8]{1,0:T(8,128)S(1)}, s32[8,8]{1,0:T(8,128)}, u32[]{:S(2)}) copy-start(s32[8,8]{1,0:T(8,128)} %param.6) | copy-start | bytes 772
  17.8 10.7 %collective-permute-start = (bf16[8,256,512]{2,1,0:T(8,128)(2,1)S(1)}, bf16[8,256,512]{2,1,0:T(8,128)(2,1)}, u32[]{:S(2)}, u32[]{:S(2)}) collective-permute-start(bf16[8,256,512]{2,1,0:T(8,128)(2,1)S(1)} %get-tuple-element.9), channel_id=1, source_target_pairs={{0,1},{1,0},{2,3},{3,2},{4,5},{5,4},{6,7},{7,6},{8,9},{9,8},{10,11... | collective-permute-start | bytes 6291464 | tf_op jit(solution)/shard_map/ppermute | solution.py:73
  18.6 9.8 %copy-start.3 = (s32[128]{0:T(128)S(1)}, s32[128]{0:T(128)}, u32[]{:S(2)}) copy-start(s32[128]{0:T(128)} %param.7) | copy-start | bytes 1540
  31.0 15.2 %collective-permute-start.1 = (bf16[2,2,128,512]{3,2,1,0:T(8,128)(2,1)S(1)}, bf16[2,2,128,512]{3,2,1,0:T(8,128)(2,1)S(1)}, u32[]{:S(2)}, u32[]{:S(2)}) collective-permute-start(bf16[2,2,128,512]{3,2,1,0:T(8,128)(2,1)S(1)} %dynamic-slice_bitcast_fusion.1), channel_id=1, source_target_pairs={{0,2},{1,3},{2,0},{3,1},{4,6},{5,7},{6,4},{7,5},{8,10},{9,11},{10,... | collective-permute-start | bytes 1572872 | tf_op jit(solution)/shard_map/ppermute | solution.py:73
  33.7 14.5 %collective-permute-start.4 = (bf16[2,2,128,512]{3,2,1,0:T(8,128)(2,1)S(1)}, bf16[2,2,128,512]{3,2,1,0:T(8,128)(2,1)S(1)}, u32[]{:S(2)}, u32[]{:S(2)}) collective-permute-start(bf16[2,2,128,512]{3,2,1,0:T(8,128)(2,1)S(1)} %dynamic-slice_bitcast_fusion), channel_id=1, source_target_pairs={{0,4},{1,5},{2,6},{3,7},{4,0},{5,1},{6,2},{7,3},{8,12},{9,13},{10,... | collective-permute-start | bytes 1572872 | tf_op jit(solution)/shard_map/ppermute | solution.py:73
  46.2 13.5 %collective-permute-start.2 = (bf16[2,128,512]{2,1,0:T(8,128)(2,1)S(1)}, bf16[2,128,512]{2,1,0:T(8,128)(2,1)S(1)}, u32[]{:S(2)}, u32[]{:S(2)}) collective-permute-start(bf16[2,128,512]{2,1,0:T(8,128)(2,1)S(1)} %dynamic-slice_bitcast_fusion.3), channel_id=1, source_target_pairs={{0,4},{1,5},{2,6},{3,7},{4,0},{5,1},{6,2},{7,3},{8,12},{9,13},{10,... | collective-permute-start | bytes 786440 | tf_op jit(solution)/shard_map/ppermute | solution.py:73
  48.2 17.2 %collective-permute-start.5 = (bf16[2,128,512]{2,1,0:T(8,128)(2,1)S(1)}, bf16[2,128,512]{2,1,0:T(8,128)(2,1)S(1)}, u32[]{:S(2)}, u32[]{:S(2)}) collective-permute-start(bf16[2,128,512]{2,1,0:T(8,128)(2,1)S(1)} %dynamic-slice_bitcast_fusion.2), channel_id=1, source_target_pairs={{0,8},{1,9},{2,10},{3,11},{4,12},{5,13},{6,14},{7,15},{8,0},{9,1},... | collective-permute-start | bytes 786440 | tf_op jit(solution)/shard_map/ppermute | solution.py:73
  59.8 8.3 %collective-permute-start.3 = (bf16[128,512]{1,0:T(8,128)(2,1)S(1)}, bf16[128,512]{1,0:T(8,128)(2,1)S(1)}, u32[]{:S(2)}, u32[]{:S(2)}) collective-permute-start(bf16[128,512]{1,0:T(8,128)(2,1)S(1)} %dynamic-slice_bitcast_fusion.5), channel_id=1, source_target_pairs={{0,8},{1,9},{2,10},{3,11},{4,12},{5,13},{6,14},{7,15},{8,0},{9,1},... | collective-permute-start | bytes 393224 | tf_op jit(solution)/shard_map/ppermute | solution.py:73
  65.5 5.0 %collective-permute-start.6 = (bf16[128,512]{1,0:T(8,128)(2,1)S(1)}, bf16[128,512]{1,0:T(8,128)(2,1)S(1)}, u32[]{:S(2)}, u32[]{:S(2)}) collective-permute-start(bf16[128,512]{1,0:T(8,128)(2,1)S(1)} %dynamic-slice_bitcast_fusion.4), channel_id=1, source_target_pairs={{0,2},{1,3},{2,0},{3,1},{4,6},{5,7},{6,4},{7,5},{8,10},{9,11},{10,... | collective-permute-start | bytes 393224 | tf_op jit(solution)/shard_map/ppermute | solution.py:73
  71.7 1.0 copy-start
  72.6 7.5 %copy-start.1 = (bf16[256,512]{1,0:T(8,128)(2,1)S(1)}, bf16[256,512]{1,0:T(8,128)(2,1)}, u32[]{:S(2)}) copy-start(bf16[256,512]{1,0:T(8,128)(2,1)} %divide_convert_fusion.panel_ref) | copy-start | bytes 786436
  80.0 9.1 %collective-permute-start.7 = (bf16[8,256,512]{2,1,0:T(8,128)(2,1)S(1)}, bf16[8,256,512]{2,1,0:T(8,128)(2,1)S(1)}, u32[]{:S(2)}, u32[]{:S(2)}) collective-permute-start(bf16[8,256,512]{2,1,0:T(8,128)(2,1)S(1)} %shard_map.63), channel_id=1, source_target_pairs={{0,1},{1,0},{2,3},{3,2},{4,5},{5,4},{6,7},{7,6},{8,9},{9,8},{10,11... | collective-permute-start | bytes 6291464 | tf_op jit(solution)/shard_map/ppermute | solution.py:73
  92.6 22.8 %collective-permute-start.11 = (bf16[2,2,128,512]{3,2,1,0:T(8,128)(2,1)S(1)}, bf16[2,2,128,512]{3,2,1,0:T(8,128)(2,1)S(1)}, u32[]{:S(2)}, u32[]{:S(2)}) collective-permute-start(bf16[2,2,128,512]{3,2,1,0:T(8,128)(2,1)S(1)} %fusion.1), channel_id=1, source_target_pairs={{0,4},{1,5},{2,6},{3,7},{4,0},{5,1},{6,2},{7,3},{8,12},{9,13},{10,... | collective-permute-start | bytes 1572872 | tf_op jit(solution)/shard_map/ppermute | solution.py:73
  94.3 25.3 %collective-permute-start.8 = (bf16[2,2,128,512]{3,2,0,1:T(8,128)(2,1)S(1)}, bf16[2,2,128,512]{3,2,0,1:T(8,128)(2,1)S(1)}, u32[]{:S(2)}, u32[]{:S(2)}) collective-permute-start(bf16[2,2,128,512]{3,2,0,1:T(8,128)(2,1)S(1)} %fusion), channel_id=1, source_target_pairs={{0,2},{1,3},{2,0},{3,1},{4,6},{5,7},{6,4},{7,5},{8,10},{9,11},{10,... | collective-permute-start | bytes 1572872 | tf_op jit(solution)/shard_map/ppermute | solution.py:73
  115.6 22.7 %collective-permute-start.12 = (bf16[2,128,512]{2,1,0:T(8,128)(2,1)S(1)}, bf16[2,128,512]{2,1,0:T(8,128)(2,1)S(1)}, u32[]{:S(2)}, u32[]{:S(2)}) collective-permute-start(bf16[2,128,512]{2,1,0:T(8,128)(2,1)S(1)} %fusion.3), channel_id=1, source_target_pairs={{0,8},{1,9},{2,10},{3,11},{4,12},{5,13},{6,14},{7,15},{8,0},{9,1},... | collective-permute-start | bytes 786440 | tf_op jit(solution)/shard_map/ppermute | solution.py:73
  119.9 19.3 %collective-permute-start.9 = (bf16[2,128,512]{2,1,0:T(8,128)(2,1)S(1)}, bf16[2,128,512]{2,1,0:T(8,128)(2,1)S(1)}, u32[]{:S(2)}, u32[]{:S(2)}) collective-permute-start(bf16[2,128,512]{2,1,0:T(8,128)(2,1)S(1)} %fusion.2), channel_id=1, source_target_pairs={{0,4},{1,5},{2,6},{3,7},{4,0},{5,1},{6,2},{7,3},{8,12},{9,13},{10,... | collective-permute-start | bytes 786440 | tf_op jit(solution)/shard_map/ppermute | solution.py:73
  138.4 5.0 %collective-permute-start.13 = (bf16[128,512]{1,0:T(8,128)(2,1)S(1)}, bf16[128,512]{1,0:T(8,128)(2,1)S(1)}, u32[]{:S(2)}, u32[]{:S(2)}) collective-permute-start(bf16[128,512]{1,0:T(8,128)(2,1)S(1)} %fusion.5), channel_id=1, source_target_pairs={{0,2},{1,3},{2,0},{3,1},{4,6},{5,7},{6,4},{7,5},{8,10},{9,11},{10,... | collective-permute-start | bytes 393224 | tf_op jit(solution)/shard_map/ppermute | solution.py:73
  139.3 7.2 %collective-permute-start.10 = (bf16[128,512]{1,0:T(8,128)(2,1)S(1)}, bf16[128,512]{1,0:T(8,128)(2,1)S(1)}, u32[]{:S(2)}, u32[]{:S(2)}) collective-permute-start(bf16[128,512]{1,0:T(8,128)(2,1)S(1)} %fusion.4), channel_id=1, source_target_pairs={{0,8},{1,9},{2,10},{3,11},{4,12},{5,13},{6,14},{7,15},{8,0},{9,1},... | collective-permute-start | bytes 393224 | tf_op jit(solution)/shard_map/ppermute | solution.py:73
Sparse Core Ops, SparseCore 0:
  71.6 67.4 all-gather.2
